TPU v7x, 256 devices: a whole 4x4x8 slice. The times are simulated.
256 devices in a mesh: fsdp: 32 (over z, y), tensor: 8 (over x, core).
Axes of the slice: x: 4, y: 4, z: 8, core: 2. Of those that a mesh axis runs over, the one named last changes fastest.
Arguments:
- context: bfloat16 [8192, 4096], P('fsdp', 'tensor'), may hold values from -6 to 6
- cotangent: bfloat16 [8192, 8192], P('fsdp', 'tensor'), may hold values from -0.0625 to 0.0625
- block_table: int32 [8, 64], P('tensor'), may hold values from 0 to 63, each once within a row
- left_stat: float32 [8, 64, 256, 256], P('tensor', 'fsdp'), may hold values from -1 to 5, as said below
- right_stat: float32 [8, 64, 256, 256], P('tensor', 'fsdp'), may hold values from -1 to 5, as said below
- root_left: float32 [8, 64, 256, 256], P('tensor', 'fsdp'), may hold values from -1 to 5, as said below
- root_right: float32 [8, 64, 256, 256], P('tensor', 'fsdp'), may hold values from -1 to 5, as said below
- second_moment: float32 [8, 64, 256, 256], P('tensor', 'fsdp'), may hold values from 0.3 to 3
Outputs:
- left_new: float32 [8, 64, 256, 256], P('tensor', 'fsdp')
- right_new: float32 [8, 64, 256, 256], P('tensor', 'fsdp')
- second_new: float32 [8, 64, 256, 256], P('tensor', 'fsdp')
- search_direction: bfloat16 [8, 512, 8192], P('tensor', 'fsdp')
Inputs may be any that keep to these rules, and one draw needn't show every extreme that they name: Each row of block_table names every block 0 to 63 once. `left_stat`: symmetric, with positive diagonal. `right_stat`: symmetric, with positive diagonal. `root_left`: symmetric, with positive diagonal. `root_right`: symmetric, with positive diagonal.
All inputs are finite; a program needn't handle non-finite values.
Results may differ from a plain program's by a relative error of at most 0.017.
Values may be sent and summed in bfloat16 or wider, within the bound.
A program may use at most 128 MiB of HBM per device.

v0:
```python
import jax
import jax.numpy as jnp
from jax import lax
from jax.sharding import Mesh
from jax.sharding import PartitionSpec as P

FSDP = ("fsdp_0", "fsdp_1")


decay_rate = 0.95


def own_rows(terms, axes):
    total = terms.astype(jnp.bfloat16)
    for axis in axes:
        total = lax.psum_scatter(total, axis, scatter_dimension=0, tiled=True)
    return total.astype(jnp.float32)


def per_device(
    context, cotangent, block_table, left_stat, right_stat, root_left, root_right, second_moment
):
    full_cot = lax.all_gather(cotangent, "tensor", axis=1, tiled=True)
    tokens_here, band_rows = context.shape
    model_width = full_cot.shape[1]
    block_size = left_stat.shape[-1]
    slot_count = left_stat.shape[1]
    groups = lax.axis_size(FSDP)
    position = lax.axis_index(FSDP)
    owner_table = block_table[0]
    col_bands = model_width // block_size
    strip_rows = band_rows // groups
    per_band = block_size // strip_rows
    my_blocks = lax.dynamic_slice_in_dim(owner_table, position * slot_count, slot_count)
    ctx_bands = context.reshape(tokens_here, band_rows // block_size, block_size)
    cot_bands = full_cot.reshape(tokens_here, col_bands, block_size)
    left_part = jnp.take(ctx_bands, owner_table // col_bands, axis=1)
    right_part = jnp.take(cot_bands, owner_table % col_bands, axis=1)
    blocks = jnp.einsum("tnb,tnc->nbc", left_part, right_part, preferred_element_type=jnp.float32)
    gradient = own_rows(
        blocks.reshape(slot_count * block_size * lax.axis_size(FSDP), block_size), FSDP
    )
    gradient = gradient.reshape(slot_count, block_size, block_size)
    highest = lax.Precision.HIGHEST
    gram_left = jnp.einsum("sij,skj->sik", gradient, gradient, precision=highest)
    gram_right = jnp.einsum("sji,sjk->sik", gradient, gradient, precision=highest)
    left_new = decay_rate * left_stat[0] + (1.0 - decay_rate) * gram_left / block_size
    right_new = decay_rate * right_stat[0] + (1.0 - decay_rate) * gram_right / block_size
    second_new = decay_rate * second_moment[0] + (1.0 - decay_rate) * gradient * gradient
    adam_step = gradient / (jnp.sqrt(second_new) + 1e-08)
    shaped = jnp.einsum("sij,sjk->sik", root_left[0], gradient, precision=highest)
    shaped = jnp.einsum("sij,sjk->sik", shaped, root_right[0], precision=highest)
    graft_ratio = jnp.sqrt(jnp.sum(adam_step * adam_step, axis=(1, 2))) / jnp.sqrt(
        jnp.sum(shaped * shaped, axis=(1, 2)) + 1e-06
    )
    direction = (shaped * graft_ratio[:, None, None]).astype(jnp.bfloat16)
    by_strip = direction.reshape(slot_count, per_band, strip_rows, block_size)
    targets = jnp.arange(groups, dtype=jnp.int32)
    chosen = jnp.take(by_strip, targets % per_band, axis=1)
    keep_mask = ((my_blocks // col_bands)[:, None] == (targets // per_band)[None, :]).astype(
        jnp.bfloat16
    )
    outgoing_rows = jnp.swapaxes(chosen * keep_mask[:, :, None, None], 0, 1)
    returned = lax.all_to_all(outgoing_rows, FSDP, split_axis=0, concat_axis=0, tiled=True)
    wanted = position // per_band * col_bands + jnp.arange(col_bands, dtype=jnp.int32)
    slot_ids = jnp.arange(owner_table.shape[0], dtype=jnp.int32)
    located = jnp.sum(
        jnp.where(owner_table[None, :] == wanted[:, None], slot_ids[None, :], 0), axis=1
    )
    flat_pieces = returned.reshape(groups * slot_count, strip_rows, block_size)
    pieces = jnp.take(flat_pieces, located, axis=0)
    result = jnp.swapaxes(pieces, 0, 1).reshape(strip_rows, model_width)
    return (left_new[None], right_new[None], second_new[None], result[None])


def solution(mesh):
    finer = Mesh(mesh.devices.reshape(8, 4, mesh.shape["tensor"]), ("fsdp_0", "fsdp_1", "tensor"))
    in_specs = (
        P(FSDP, "tensor"),
        P(FSDP, "tensor"),
        P("tensor", None),
        P("tensor", FSDP, None, None),
        P("tensor", FSDP, None, None),
        P("tensor", FSDP, None, None),
        P("tensor", FSDP, None, None),
        P("tensor", FSDP, None, None),
    )
    out_specs = (
        P("tensor", FSDP, None, None),
        P("tensor", FSDP, None, None),
        P("tensor", FSDP, None, None),
        P("tensor", FSDP, None),
    )
    return jax.shard_map(
        per_device, mesh=finer, in_specs=in_specs, out_specs=out_specs, check_vma=False
    )
```

profile of v0, /device:TPU:32, one launch (start us, length us, event | category | flops | bytes accessed | tf_op | source)
XLA Modules:
  0.0 235.5 jit_solution(10105942067028597240)
XLA Ops:
  7.2 0.0 copy-start
  7.2 0.0 all-gather.2.cloned.1.call-start
  7.2 2.1 copy.38
  9.3 0.0 all-gather.2.cloned.1.call-update
  9.3 0.0 reduce-scatter.3.cloned.1.call-start
  9.4 1.1 copy.36
  10.5 0.1 copy.37
  10.6 0.7 fusion.28
  11.3 0.0 copy-start.6
  11.3 5.3 %gather_fusion = bf16[64,256,256]{2,1,0:T(8,128)(2,1)} fusion(bf16[256,2,256]{2,0,1:T(8,128)(2,1)S(1)} %copy.37, s32[1024]{0:T(1024)S(1)} %get-tuple-element.13), kind=kCustom, calls=%fused_computation | custom fusion | bytes 16777472 | tf_op jit(solution)/shard_map/jit(_take)/gather | solution.py:37
  16.7 0.0 copy-done.6
  16.7 31.0 %all-gather.2.cloned.1.call-done = bf16[256,8192]{0,1:T(8,128)(2,1)} async-done(((bf16[256,1024]{0,1:T(8,128)(2,1)}), bf16[256,8192]{0,1:T(8,128)(2,1)}) %all-gather.2.cloned.1.call-update) | async-done | bytes 4194320 | tf_op jit(solution)/shard_map/all_gather | solution.py:23
  47.6 6.4 %copy.39 = bf16[256,32,256]{2,0,1:T(8,128)(2,1)} copy(bf16[256,32,256]{0,2,1:T(8,128)(2,1)} %bitcast.93) | data formatting | bytes 8388608 | tf_op jit(solution)/shard_map/reshape | solution.py:36
  54.1 7.7 %gather_fusion.1 = bf16[64,256,256]{2,1,0:T(8,128)(2,1)} fusion(bf16[256,32,256]{2,0,1:T(8,128)(2,1)} %copy.39, s32[1024]{0:T(1024)S(1)} %get-tuple-element.12), kind=kCustom, calls=%fused_computation.1 | custom fusion | bytes 16777472 | tf_op jit(solution)/shard_map/jit(_take)/gather | solution.py:38
  61.8 11.4 %fusion.7 = bf16[64,256,256]{2,1,0:T(8,128)(2,1)} fusion(bf16[64,256,256]{2,1,0:T(8,128)(2,1)} %gather_fusion.1, pred[64]{0:T(512)(128)(4,1)S(1)} %get-tuple-element.7, bf16[64,256,256]{2,1,0:T(8,128)(2,1)} %gather_fusion, pred[64]{0:T(512)(128)(4,1)S(1)} %get-tuple-element.6), kind=kOutput, calls=%fused_computation.11 | convolution fusion | flops 2160066560 | bytes 25165952 | tf_op jit(solution)/shard_map/tnb,tnc->nbc/dot_general | solution.py:39
  73.1 0.0 copy-start.2
  73.2 0.0 copy-start.4
  73.2 0.0 reduce-scatter.3.cloned.1.call-update
  73.2 0.0 reduce-scatter.5.cloned.1.call-start
  73.2 93.3 %reduce-scatter.3.cloned.1.call-done = bf16[2048,256]{1,0:T(8,128)(2,1)} async-done(((bf16[16384,256]{1,0:T(8,128)(2,1)}), bf16[2048,256]{1,0:T(8,128)(2,1)}) %reduce-scatter.3.cloned.1.call-update) | async-done | bytes 1048592 | tf_op jit(solution)/shard_map/reduce_scatter | solution.py:16
  166.5 0.0 reduce-scatter.5.cloned.1.call-update
  166.6 0.1 and_select_fusion.1
  166.6 0.1 compare_convert_fusion
  166.7 0.1 copy.44
  166.8 29.0 %reduce-scatter.5.cloned.1.call-done = bf16[512,256]{1,0:T(8,128)(2,1)} async-done(((bf16[2048,256]{1,0:T(8,128)(2,1)}), bf16[512,256]{1,0:T(8,128)(2,1)}) %reduce-scatter.5.cloned.1.call-update) | async-done | bytes 262160 | tf_op jit(solution)/shard_map/reduce_scatter | solution.py:16
  195.8 0.0 copy-done.2
  195.8 1.9 broadcast_multiply_fusion
  197.7 1.3 fusion.27
  199.1 0.0 copy-done.5
  199.1 1.3 fusion.25
  200.5 0.0 copy-done
  200.5 0.8 multiply_reduce_fusion
  201.2 0.1 reduce_sum.39
  201.4 0.1 multiply_convert_fusion
  201.5 0.6 gather_fusion.2
  202.1 1.0 select_multiply_fusion
  203.0 8.5 %all-to-all-start = ((bf16[32,2,16,256]{3,2,1,0:T(8,128)(2,1)}), bf16[32,2,16,256]{3,2,1,0:T(8,128)(2,1)S(1)}, u32[]{:S(2)}, u32[]{:S(2)}) async-start(bf16[32,2,16,256]{3,2,1,0:T(8,128)(2,1)} %select_multiply_fusion), calls=%async_computation.2 | async-start | bytes 1048576 | tf_op jit(solution)/shard_map/all_to_all | solution.py:64
  211.6 0.2 select_reduce_fusion
  211.8 0.0 copy-done.3
  211.8 0.0 copy-done.1
  211.8 1.1 fusion.14
  212.9 0.0 copy-done.4
  212.9 1.1 fusion.16
  214.0 13.4 %all-to-all-done = bf16[32,2,16,256]{3,2,1,0:T(8,128)(2,1)S(1)} async-done(((bf16[32,2,16,256]{3,2,1,0:T(8,128)(2,1)}), bf16[32,2,16,256]{3,2,1,0:T(8,128)(2,1)S(1)}, u32[]{:S(2)}, u32[]{:S(2)}) %all-to-all-start) | async-done | bytes 524320 | tf_op jit(solution)/shard_map/all_to_all | solution.py:64
  227.3 0.6 gather_fusion.3
  227.9 0.1 select_bitcast_fusion
  228.0 0.1 copy.45
  228.1 0.8 broadcast_in_dim_reshape.3
  (15 shorter events, 0.1 us)
Async XLA Ops:
  7.2 193.3 %copy-start = (f32[1,2,256,256]{3,2,1,0:T(8,128)S(1)}, f32[1,2,256,256]{3,2,1,0:T(8,128)}, u32[]{:S(2)}) copy-start(f32[1,2,256,256]{3,2,1,0:T(8,128)} %param.14) | copy-start | bytes 1572868
  7.2 40.5 %all-gather.2.cloned.1.call-start = ((), (), s32[]{:S(2)}) async-start(), calls=%async_computation.3 | async-start | bytes 4718592 | tf_op jit(solution)/shard_map/all_gather | solution.py:23
  9.3 157.2 %reduce-scatter.3.cloned.1.call-start = ((), (), s32[]{:S(2)}) async-start(), calls=%async_computation.4 | async-start | bytes 9437184 | tf_op jit(solution)/shard_map/reduce_scatter | solution.py:16
  11.3 5.4 %copy-start.6 = (s32[1,64]{1,0:T(1,128)S(1)}, s32[1,64]{1,0:T(1,128)}, u32[]{:S(2)}) copy-start(s32[1,64]{1,0:T(1,128)} %param.10) | copy-start | bytes 772
  73.1 122.7 %copy-start.2 = (f32[1,2,256,256]{3,2,1,0:T(8,128)S(1)}, f32[1,2,256,256]{3,2,1,0:T(8,128)}, u32[]{:S(2)}) copy-start(f32[1,2,256,256]{3,2,1,0:T(8,128)} %param.15) | copy-start | bytes 1572868
  73.1 126.0 %copy-start.5 = (f32[1,2,256,256]{3,2,1,0:T(8,128)S(1)}, f32[1,2,256,256]{3,2,1,0:T(8,128)}, u32[]{:S(2)}) copy-start(f32[1,2,256,256]{3,2,1,0:T(8,128)} %param.13) | copy-start | bytes 1572868
  73.1 138.7 %copy-start.3 = (f32[1,2,256,256]{3,2,1,0:T(8,128)S(1)}, f32[1,2,256,256]{3,2,1,0:T(8,128)}, u32[]{:S(2)}) copy-start(f32[1,2,256,256]{3,2,1,0:T(8,128)} %param.12) | copy-start | bytes 1572868
  73.2 139.7 %copy-start.4 = (f32[1,2,256,256]{3,2,1,0:T(8,128)S(1)}, f32[1,2,256,256]{3,2,1,0:T(8,128)}, u32[]{:S(2)}) copy-start(f32[1,2,256,256]{3,2,1,0:T(8,128)} %param.11) | copy-start | bytes 1572868
  73.2 122.6 %reduce-scatter.5.cloned.1.call-start = ((), (), s32[]{:S(2)}) async-start(), calls=%async_computation.5 | async-start | bytes 1310720 | tf_op jit(solution)/shard_map/reduce_scatter | solution.py:16
  195.8 16.0 %copy-start.1 = (bf16[512,256]{1,0:T(8,128)(2,1)S(1)}, bf16[512,256]{1,0:T(8,128)(2,1)}, u32[]{:S(2)}) copy-start(bf16[512,256]{1,0:T(8,128)(2,1)} %reduce-scatter.5.cloned.1.call-done) | copy-start | bytes 786436
  203.0 24.3 %all-to-all-start = ((bf16[32,2,16,256]{3,2,1,0:T(8,128)(2,1)}), bf16[32,2,16,256]{3,2,1,0:T(8,128)(2,1)S(1)}, u32[]{:S(2)}, u32[]{:S(2)}) async-start(bf16[32,2,16,256]{3,2,1,0:T(8,128)(2,1)} %select_multiply_fusion), calls=%async_computation.2 | async-start | bytes 1048576 | tf_op jit(solution)/shard_map/all_to_all | solution.py:64
Sparse Core Ops, SparseCore 0:
  10.4 37.1 all-gather.1
  73.3 93.1 reduce-scatter.2
  169.1 26.7 reduce-scatter.4
where the time goes:
time: 237 us; the launch traced here: 235 us
  waiting for transfers between devices  167 us (70%)
  local copies, waits for them, and re-layouts  25 us (11%)
  matrix products  15.6 us (7%)
  between operations  13.9 us (6%)
  starting transfers between devices  8.67 us (4%)
  other arithmetic  5.64 us (2%)
    reduce_scatter x2, waiting for transfers between devices, own_rows(): total = lax.psum_scatter(total, axis, scatter_dimension=0, tiled=True)  122 us
    all_gather x1, waiting for transfers between devices, per_device(): full_cot = lax.all_gather(cotangent, 'tensor', axis=1, tiled=True)  31 us
    all_to_all x1, waiting for transfers between devices, per_device(): lax.all_to_all(outgoing_rows, FSDP, split_axis=0, concat_axis=0, tiled=True)  13.4 us
    dot_general x1, matrix products, per_device(): jnp.einsum('tnb,tnc->nbc', left_part, right_part, preferred_element_type=...  11.4 us
    all_to_all x1, starting transfers between devices, per_device(): lax.all_to_all(outgoing_rows, FSDP, split_axis=0, concat_axis=0, tiled=True)  8.55 us
    gather x1, local copies, waits for them, and re-layouts, per_device(): right_part = jnp.take(cot_bands, owner_table % col_bands, axis=1)  7.71 us
    reshape x1, local copies, waits for them, and re-layouts, per_device(): cot_bands = full_cot.reshape(tokens_here, col_bands, block_size)  6.43 us
    gather x1, local copies, waits for them, and re-layouts, per_device(): left_part = jnp.take(ctx_bands, owner_table // col_bands, axis=1)  5.35 us
  transfers between devices with their start and end apart: 4, of which 4 were waited for; matrix products, arithmetic and copies ran while one was open for 4% of the time, Pallas kernels for 0%

commit v1 on v0

v1 whole, which is shorter than its diff:
```python
import functools

import jax
import jax.numpy as jnp
from jax import lax
from jax.experimental import pallas as pl
from jax.experimental.pallas import tpu as pltpu
from jax.sharding import Mesh
from jax.sharding import PartitionSpec as P

MESH = pl.DeviceIdType.MESH
bf16 = jnp.bfloat16
f32 = jnp.float32
decay_rate = 0.95

NZ, NY, NX = 8, 4, 4
TOK = 256
BLOCK = 256
BAND = 512
COLS = 1024
PATCH = BLOCK // NY
QC = COLS // NY
STRIP = BLOCK // NZ
Y_OFF = (0, -1, 1, 2)
X_OFF = (0, -1, 1, 2)


class Names:
    def __init__(self):
        self.ids = {}

    def __call__(self, *name):
        return self.ids.setdefault(name, len(self.ids))


N_SEND, N_RECV = 160, 128


def kernel(
    ctx, cot, tbl, inv, ls, rs, rl, rr, sm,
    ln, rn, sn, sd,
    pieces, relay, bq, aall, cbuf, zr, summed, out1, in1, grad, dirs, in2, rows,
    ls_v, rs_v, rl_v, rr_v, sm_v,
    send_sems, recv_sems, a1s, a1r, a2s, a2r, loc,
):
    x, y, z, c = (lax.axis_index(n) for n in ("x", "y", "z", "c"))
    me = z * NY + y
    t_me = x * 2 + c
    started = []
    sid, rid = Names(), Names()

    def wrap(v, n):
        return lax.rem(v + n, n)

    def send(src, dst, name, **where):
        k = sid(len(started))
        copy = pltpu.make_async_remote_copy(
            src_ref=src, dst_ref=dst,
            send_sem=send_sems.at[k], recv_sem=recv_sems.at[rid(*name)],
            device_id=where, device_id_type=MESH,
        )
        copy.start()
        started.append(copy)

    def arrived(dst, *name):
        pltpu.make_async_remote_copy(
            src_ref=dst, dst_ref=dst,
            send_sem=send_sems.at[0], recv_sem=recv_sems.at[rid(*name)],
            device_id={"c": 1 - c}, device_id_type=MESH,
        ).wait_recv()

    yp, ym, y2 = wrap(y + 1, NY), wrap(y - 1, NY), wrap(y + 2, NY)
    xp, xm = wrap(x + 1, NX), wrap(x - 1, NX)
    zp, zm = wrap(z + 1, NZ), wrap(z - 1, NZ)

    stats = [
        pltpu.make_async_copy(a, b, loc.at[i])
        for i, (a, b) in enumerate(((rl, rl_v), (rr, rr_v), (sm, sm_v), (ls, ls_v), (rs, rs_v)))
    ]

    barrier = pltpu.get_barrier_semaphore()
    for where in ({"y": yp}, {"y": ym}, {"x": xp}, {"x": xm}, {"z": zp}, {"z": zm}, {"c": 1 - c}):
        pl.semaphore_signal(barrier, inc=1, device_id=where, device_id_type=MESH)

    src_col = lax.broadcasted_iota(jnp.int32, (512, 512), 0)
    q = lax.broadcasted_iota(jnp.int32, (512, 512), 1)
    lane = lax.rem(q, 128)
    y_of = lax.rem(q // 128 + y, NY)
    pick = (src_col == (lane // PATCH) * BLOCK + PATCH * y_of + lax.rem(lane, PATCH)).astype(f32).astype(bf16)
    for j in range(2):
        got = jnp.dot(cot[:, 512 * j : 512 * j + 512], pick, preferred_element_type=f32).astype(bf16)
        for r in range(NY):
            pieces[r, :, 128 * j : 128 * j + 128] = got[:, 128 * r : 128 * r + 128]

    def bpart(t, ya, half=None):
        if half is None:
            return bq.at[t, pl.ds(ya * TOK, TOK)]
        return bq.at[t, pl.ds(ya * TOK + half * (TOK // 2), TOK // 2)]

    pl.semaphore_wait(barrier, 7)

    here = bpart(t_me, y)
    send(pieces.at[1], here, ("By", -1), y=yp)
    send(pieces.at[3], here, ("By", 1), y=ym)
    send(pieces.at[2, pl.ds(0, TOK // 2)], relay.at[0], ("Rb", 0), y=yp)
    send(pieces.at[2, pl.ds(TOK // 2, TOK // 2)], relay.at[1], ("Rb", 1), y=ym)
    send(pieces.at[0], here, ("Bx", -1, 0), x=xp)
    send(pieces.at[0], here, ("Bx", 1, 0), x=xm)
    send(pieces.at[0], here, ("Bc", 0, 0), c=1 - c)
    for copy in stats:
        copy.start()
    bq[t_me, pl.ds(y * TOK, TOK)] = pieces[0]

    turned = ctx[...].astype(f32).T.astype(bf16)
    lanes = pl.ds(pl.multiple_of(y * TOK, TOK), TOK)
    for zz in range(NZ):
        for h in range(2):
            aall[zz * 64 + h * 32 : zz * 64 + h * 32 + 32, lanes] = turned[
                h * 256 + zz * 32 : h * 256 + zz * 32 + 32
            ]

    def apart(ya, half=None):
        cols = pl.ds(pl.multiple_of(ya * TOK, TOK), TOK)
        if half is None:
            return aall.at[:, cols]
        return aall.at[pl.ds(half * 256, 256), cols]

    send(apart(y), apart(y), ("Ay", -1), y=yp)
    send(apart(y), apart(y), ("Ay", 1), y=ym)

    def spread(yi):
        part = bpart(t_me, wrap(y + Y_OFF[yi], NY))
        send(part, part, ("Bx", -1, yi), x=xp)
        send(part, part, ("Bx", 1, yi), x=xm)
        send(part, part, ("Bc", 0, yi), c=1 - c)

    arrived(here, "By", -1)
    spread(1)
    arrived(here, "By", 1)
    spread(2)
    arrived(relay.at[0], "Rb", 0)
    send(relay.at[0], bpart(t_me, ym, 0), ("By2", 0), y=yp)
    arrived(relay.at[1], "Rb", 1)
    send(relay.at[1], bpart(t_me, yp, 1), ("By2", 1), y=ym)

    def pass_on(yi):
        ya = wrap(y + Y_OFF[yi], NY)
        for off, x_at, half, to in ((-1, xm, 0, xp), (1, xp, 1, xm)):
            t = x_at * 2 + c
            arrived(bpart(t, ya), "Bx", off, yi)
            send(bpart(t, ya, half), bpart(t, ya, half), ("Bx2", half, yi), x=to)
            send(bpart(t, ya), bpart(t, ya), ("Bc", off, yi), c=1 - c)

    pass_on(0)
    arrived(bpart(t_me, y2, 0), "By2", 0)
    arrived(bpart(t_me, y2, 1), "By2", 1)
    spread(3)
    arrived(apart(ym), "Ay", -1)
    send(apart(ym, 0), apart(ym, 0), ("Ay2", 0), y=yp)
    arrived(apart(yp), "Ay", 1)
    send(apart(yp, 1), apart(yp, 1), ("Ay2", 1), y=ym)
    pass_on(1)
    pass_on(2)
    arrived(apart(y2, 0), "Ay2", 0)
    arrived(apart(y2, 1), "Ay2", 1)

    def product(g):
        off = X_OFF[g]
        xa = wrap(x + off, NX)
        for yi in range(NY):
            arrived(here, "Bc", off, yi)

        def one(cc, carry):
            total = jnp.dot(aall[...], bq[xa * 2 + cc], preferred_element_type=f32)
            cbuf[g, :, :, pl.ds(pl.multiple_of(cc * QC, QC), QC)] = total.astype(bf16).reshape(NZ, 64, QC)
            return carry

        lax.fori_loop(0, 2, one, 0)

    half_rows = (pl.ds(0, 32), pl.ds(32, 32))

    def step(g, s):
        dist = 5 - s
        for d, sign, to in ((0, 1, zp), (1, -1, zm)):
            zd = wrap(z + sign * dist, NZ)
            name = ("Z", g, d, s)
            if s == 1:
                send(cbuf.at[g, zd, half_rows[d]], zr.at[g, d, 0, half_rows[d]], name, z=to)
                continue
            if s == 2:
                arrived(zr.at[g, d, 0, half_rows[d]], "Z", g, d, 1)
                cbuf[g, zd, half_rows[d]] = (
                    cbuf[g, zd, half_rows[d]].astype(f32) + zr[g, d, 0, half_rows[d]].astype(f32)
                ).astype(bf16)
            else:
                arrived(zr.at[g, d, s - 2], "Z", g, d, s - 1)
                cbuf[g, zd] = (cbuf[g, zd].astype(f32) + zr[g, d, s - 2].astype(f32)).astype(bf16)
            send(cbuf.at[g, zd], zr.at[g, d, s - 1], name, z=to)

    def last(g):
        xa = wrap(x + X_OFF[g], NX)
        arrived(zr.at[g, 0, 3], "Z", g, 0, 4)
        arrived(zr.at[g, 1, 3], "Z", g, 1, 4)
        whole = cbuf[g, z].astype(f32) + zr[g, 0, 3].astype(f32) + zr[g, 1, 3].astype(f32)
        for k in range(4):
            tile = whole[:, 128 * k : 128 * k + 128]
            summed[xa * 4 + k, 0] = tile[:32]
            summed[xa * 4 + k, 1] = tile[32:]

    product(0)
    step(0, 1)
    pass_on(3)
    product(1)
    step(1, 1)
    product(2)
    step(2, 1)
    for g in range(3):
        step(g, 2)
    for yi in range(NY):
        t = wrap(x + 2, NX) * 2 + c
        ya = wrap(y + Y_OFF[yi], NY)
        arrived(bpart(t, ya, 0), "Bx2", 0, yi)
        arrived(bpart(t, ya, 1), "Bx2", 1, yi)
        send(bpart(t, ya), bpart(t, ya), ("Bc", 2, yi), c=1 - c)
    step(0, 3)
    product(3)
    step(3, 1)
    step(1, 3)
    step(2, 3)
    step(3, 2)
    step(0, 4)
    step(1, 4)
    step(2, 4)
    step(3, 3)
    step(3, 4)
    for g in range(4):
        last(g)

    left_lanes = lax.broadcasted_iota(jnp.int32, (16, 128), 1) < 64

    def patches(f, slot_of):
        for s in range(2):
            k = tbl[0, 2 * f + s]
            col = k & 31
            tile = summed[col >> 1, k >> 5]
            odd = (col & 1) == 1
            upper, lower = tile[:16], tile[16:]
            up_turned, low_turned = pltpu.roll(upper, 64, 1), pltpu.roll(lower, 64, 1)
            first = jnp.where(odd, up_turned, upper)
            second = jnp.where(odd, lower, low_turned)
            slot_of(s, jnp.where(left_lanes, first, second).astype(bf16))

    def far_order(i):
        dz, dy = i // NY, lax.rem(i, NY)
        zd = lax.rem(z + dz, NZ)
        yd = lax.rem(y + dy, NY)
        return zd, yd, zd * NY + yd

    def copy1(i):
        zd, yd, f = far_order(i)
        return pltpu.make_async_remote_copy(
            src_ref=out1.at[i], dst_ref=in1.at[me], send_sem=a1s.at[i], recv_sem=a1r.at[i],
            device_id={"z": zd, "y": yd}, device_id_type=MESH,
        )

    def send1(i, carry):
        zd, yd, f = far_order(i)

        def put(s, v):
            out1[i, s] = v

        patches(f, put)
        copy1(i).start()
        return carry

    lax.fori_loop(1, 32, send1, 0)

    def put_own(s, v):
        in1[me, s] = v

    patches(me, put_own)

    def wait1(i, carry):
        copy1(i).wait_recv()
        return carry

    lax.fori_loop(1, 32, wait1, 0)

    for s in range(2):
        for j in range(2):
            for zz in range(NZ):
                a = in1[zz * NY + 2 * j, s].astype(f32)
                b = in1[zz * NY + 2 * j + 1, s].astype(f32)
                at = pl.ds(128 * j, 128)
                grad[s, 32 * zz : 32 * zz + 16, at] = jnp.where(left_lanes, a, pltpu.roll(b, 64, 1))
                grad[s, 32 * zz + 16 : 32 * zz + 32, at] = jnp.where(left_lanes, pltpu.roll(a, 64, 1), b)

    highest = lax.Precision.HIGHEST
    for copy in stats[:3]:
        copy.wait()
    for s in range(2):
        g = grad[s]
        second = decay_rate * sm_v[s] + (1.0 - decay_rate) * g * g
        sm_v[s] = second
        adam = g / (jnp.sqrt(second) + 1e-08)
        shaped = jnp.dot(rl_v[s], g, precision=highest, preferred_element_type=f32)
        shaped = jnp.dot(shaped, rr_v[s], precision=highest, preferred_element_type=f32)
        ratio = jnp.sqrt(jnp.sum(adam * adam, keepdims=True)) / jnp.sqrt(
            jnp.sum(shaped * shaped, keepdims=True) + 1e-06
        )
        dirs[:, s] = (shaped * ratio).astype(bf16).reshape(16, 16, BLOCK)

    def copy2(i):
        zd, yd, f = far_order(i)
        return pltpu.make_async_remote_copy(
            src_ref=dirs.at[lax.rem(f, 16)], dst_ref=in2.at[me], send_sem=a2s.at[i], recv_sem=a2r.at[i],
            device_id={"z": zd, "y": yd}, device_id_type=MESH,
        )

    def send2(i, carry):
        copy2(i).start()
        return carry

    lax.fori_loop(1, 32, send2, 0)
    in2[me] = dirs[lax.rem(me, 16)]

    out_sn = pltpu.make_async_copy(sm_v, sn, loc.at[5])
    out_sn.start()
    for copy in stats[3:]:
        copy.wait()
    for s in range(2):
        g = grad[s].astype(bf16)
        left = lax.dot_general(g, g, (((1,), (1,)), ((), ())), preferred_element_type=f32)
        ls_v[s] = decay_rate * ls_v[s] + (1.0 - decay_rate) * left / BLOCK
        right = lax.dot_general(g, g, (((0,), (0,)), ((), ())), preferred_element_type=f32)
        rs_v[s] = decay_rate * rs_v[s] + (1.0 - decay_rate) * right / BLOCK
    out_ln = pltpu.make_async_copy(ls_v, ln, loc.at[6])
    out_rn = pltpu.make_async_copy(rs_v, rn, loc.at[7])
    out_ln.start()
    out_rn.start()

    def wait2(i, carry):
        copy2(i).wait_recv()
        return carry

    lax.fori_loop(1, 32, wait2, 0)
    half = me // 16
    for col in range(32):
        p = inv[0, half * 32 + col]
        rows[:, BLOCK * col : BLOCK * col + BLOCK] = in2[p >> 1, p & 1]
    out_sd = pltpu.make_async_copy(rows, sd, loc.at[8])
    out_sd.start()

    for copy in started:
        copy.wait_send()

    def drain(i, carry):
        copy1(i).wait_send()
        copy2(i).wait_send()
        return carry

    lax.fori_loop(1, 32, drain, 0)
    for copy in (out_sn, out_ln, out_rn, out_sd):
        copy.wait()


def per_device(context, cotangent, block_table, left_stat, right_stat, root_left, root_right, second_moment):
    ids = jnp.arange(64, dtype=jnp.int32)
    inverse = jnp.sum(jnp.where(block_table[0][None, :] == ids[:, None], ids[None, :], 0), axis=1)[None]
    vmem = pl.BlockSpec(memory_space=pltpu.VMEM)
    smem = pl.BlockSpec(memory_space=pltpu.SMEM)
    hbm = pl.BlockSpec(memory_space=pl.ANY)
    block = jax.ShapeDtypeStruct((2, BLOCK, BLOCK), f32)
    V = pltpu.VMEM
    DMA = pltpu.SemaphoreType.DMA
    ln, rn, sn, sd = pl.pallas_call(
        kernel,
        out_shape=(block, block, block, jax.ShapeDtypeStruct((16, 8192), bf16)),
        in_specs=[vmem, vmem, smem, smem, hbm, hbm, hbm, hbm, hbm],
        out_specs=(hbm, hbm, hbm, hbm),
        scratch_shapes=[
            V((NY, TOK, QC), bf16),
            V((2, TOK // 2, QC), bf16),
            V((8, NY * TOK, QC), bf16),
            V((BAND, NY * TOK), bf16),
            V((4, NZ, 64, 2 * QC), bf16),
            V((4, 2, 4, 64, 2 * QC), bf16),
            V((16, 2, 32, 128), f32),
            V((32, 2, 16, 128), bf16),
            V((32, 2, 16, 128), bf16),
            V((2, BLOCK, BLOCK), f32),
            V((16, 2, 16, BLOCK), bf16),
            V((32, 2, 16, BLOCK), bf16),
            V((16, 8192), bf16),
            *[V((2, BLOCK, BLOCK), f32)] * 5,
            DMA((N_SEND,)),
            DMA((N_RECV,)),
            DMA((32,)),
            DMA((32,)),
            DMA((32,)),
            DMA((32,)),
            DMA((9,)),
        ],
        compiler_params=pltpu.CompilerParams(collective_id=0, has_side_effects=True, vmem_limit_bytes=48 << 20),
        name="shampoo",
    )(
        context, cotangent, block_table, inverse,
        left_stat[0], right_stat[0], root_left[0], root_right[0], second_moment[0],
    )
    return ln[None], rn[None], sn[None], sd[None]


def solution(mesh):
    finer = Mesh(mesh.devices.reshape(NZ, NY, NX, 2), ("z", "y", "x", "c"))
    F, T = ("z", "y"), ("x", "c")
    stat = P(T, F, None, None)
    return jax.shard_map(
        per_device,
        mesh=finer,
        in_specs=(P(F, T), P(F, T), P(T, None), stat, stat, stat, stat, stat),
        out_specs=(stat, stat, stat, P(T, F, None)),
        check_vma=False,
    )
```

time: 237 us -> 96 us (0.41)
  waiting for transfers between devices: 167 us -> 0 us
  Pallas kernels: 0 us -> 83.2 us
  matrix products: 15.6 us -> 0 us
  local copies, waits for them, and re-layouts: 25 us -> 10.9 us
  between operations: 13.9 us -> 0.66 us
  starting transfers between devices: 8.67 us -> 0 us
  other arithmetic: 5.64 us -> 0.11 us
    reduce_scatter x2 -> x0, waiting for transfers between devices: 122 us -> none  [own_rows(): total = lax.psum_scatter(total, axis, scatter_dimension=0, tiled=True)]
    pallas_call x0 -> x1, Pallas kernels: none -> 83.2 us  [per_device(): pl.pallas_call(kernel, out_shape=(block, block, block, jax.ShapeDtypeStru...]
    all_gather x1 -> x0, waiting for transfers between devices: 31 us -> none  [per_device(): full_cot = lax.all_gather(cotangent, 'tensor', axis=1, tiled=True)]
    dot_general x5 -> x0, matrix products: 15.6 us -> none  [the longest x1 11.4 us: per_device(): jnp.einsum('tnb,tnc->nbc', left_part, right_part, preferred_element_type=...]
    gather x4 -> x0, local copies, waits for them, and re-layouts: 14.2 us -> none  [the longest x1 7.71 us: per_device(): right_part = jnp.take(cot_bands, owner_table % col_bands, axis=1)]
    all_to_all x1 -> x0, waiting for transfers between devices: 13.4 us -> none  [per_device(): lax.all_to_all(outgoing_rows, FSDP, split_axis=0, concat_axis=0, tiled=True)]
    all_to_all x1 -> x0, starting transfers between devices: 8.55 us -> none  [per_device(): lax.all_to_all(outgoing_rows, FSDP, split_axis=0, concat_axis=0, tiled=True)]
    unnamed x16 -> x20, local copies, waits for them, and re-layouts: 3.21 us -> 10.9 us
  transfers between devices with their start and end apart: 4 -> 0, of which waited for: 4 -> 0; matrix products, arithmetic and copies ran while one was open for 4% -> 0% of each run, Pallas kernels for 0% -> 0%
where the time goes in v1:
time: 96 us; the launch traced here: 94.9 us
  Pallas kernels  83.2 us (87%)
  local copies, waits for them, and re-layouts  10.9 us (11%)
    pallas_call x1, Pallas kernels, per_device(): pl.pallas_call(kernel, out_shape=(block, block, block, jax.ShapeDtypeStru...  83.2 us
    unnamed x20, local copies, waits for them, and re-layouts  10.9 us

profile of v1, /device:TPU:32, one launch (start us, length us, event | category | flops | bytes accessed | tf_op | source)
XLA Modules:
  0.0 94.9 jit_solution(3796417648227581835)
XLA Ops:
  0.6 0.0 copy-start.7
  0.6 0.6 copy-done.7
  1.3 0.1 select_reduce_fusion
  1.4 0.0 copy-start
  1.4 1.0 %copy-done = bf16[256,1024]{1,0:T(8,128)(2,1)S(1)} copy-done((bf16[256,1024]{1,0:T(8,128)(2,1)S(1)}, bf16[256,1024]{1,0:T(8,128)(2,1)}, u32[]{:S(2)}) %copy-start) | copy-done | bytes 524312
  2.4 0.0 copy-start.1
  2.4 1.0 %copy-done.1 = f32[1,2,256,256]{3,2,1,0:T(8,128)S(1)} copy-done((f32[1,2,256,256]{3,2,1,0:T(8,128)S(1)}, f32[1,2,256,256]{3,2,1,0:T(8,128)}, u32[]{:S(2)}) %copy-start.1) | copy-done | bytes 524312
  3.5 0.0 copy-start.2
  3.5 1.0 %copy-done.2 = f32[1,2,256,256]{3,2,1,0:T(8,128)S(1)} copy-done((f32[1,2,256,256]{3,2,1,0:T(8,128)S(1)}, f32[1,2,256,256]{3,2,1,0:T(8,128)}, u32[]{:S(2)}) %copy-start.2) | copy-done | bytes 524312
  4.5 0.0 copy-start.3
  4.5 1.0 %copy-done.3 = f32[1,2,256,256]{3,2,1,0:T(8,128)S(1)} copy-done((f32[1,2,256,256]{3,2,1,0:T(8,128)S(1)}, f32[1,2,256,256]{3,2,1,0:T(8,128)}, u32[]{:S(2)}) %copy-start.3) | copy-done | bytes 524312
  5.6 0.0 copy-start.4
  5.6 1.0 %copy-done.4 = f32[1,2,256,256]{3,2,1,0:T(8,128)S(1)} copy-done((f32[1,2,256,256]{3,2,1,0:T(8,128)S(1)}, f32[1,2,256,256]{3,2,1,0:T(8,128)}, u32[]{:S(2)}) %copy-start.4) | copy-done | bytes 524312
  6.6 0.0 copy-start.5
  6.6 1.0 %copy-done.5 = f32[1,2,256,256]{3,2,1,0:T(8,128)S(1)} copy-done((f32[1,2,256,256]{3,2,1,0:T(8,128)S(1)}, f32[1,2,256,256]{3,2,1,0:T(8,128)}, u32[]{:S(2)}) %copy-start.5) | copy-done | bytes 524312
  7.7 0.0 copy-start.6
  7.7 0.9 copy-done.6
  8.6 83.2 %shampoo.1 = (f32[2,256,256]{2,1,0:T(8,128)S(1)}, f32[2,256,256]{2,1,0:T(8,128)S(1)}, f32[2,256,256]{2,1,0:T(8,128)S(1)}, bf16[16,8192]{1,0:T(8,128)(2,1)S(1)}) custom-call(bf16[256,512]{1,0:T(8,128)(2,1)S(1)} %copy-done.6, bf16[256,1024]{1,0:T(8,128)(2,1)S(1)} %copy-done, s32[1,64]{1,0:T(1,128)S(1)} %copy-done.7, s32[1,64]{1,0:T(1,128)S(1)} %bitcast.21, ...), custom_call_target="tpu_custom_call" | custom-call | tf_op jit(solution)/shard_map/shampoo/pallas_call | solution.py:376
  91.8 0.8 copy.16
  92.6 0.8 copy.17
  93.4 0.8 copy.18
  94.2 0.7 copy.19
Async XLA Ops:
  0.6 0.7 copy-start.7
  1.4 1.1 %copy-start = (bf16[256,1024]{1,0:T(8,128)(2,1)S(1)}, bf16[256,1024]{1,0:T(8,128)(2,1)}, u32[]{:S(2)}) copy-start(bf16[256,1024]{1,0:T(8,128)(2,1)} %cot.1) | copy-start | bytes 1572868
  2.4 1.0 %copy-start.1 = (f32[1,2,256,256]{3,2,1,0:T(8,128)S(1)}, f32[1,2,256,256]{3,2,1,0:T(8,128)}, u32[]{:S(2)}) copy-start(f32[1,2,256,256]{3,2,1,0:T(8,128)} %param.11) | copy-start | bytes 1572868
  3.5 1.0 %copy-start.2 = (f32[1,2,256,256]{3,2,1,0:T(8,128)S(1)}, f32[1,2,256,256]{3,2,1,0:T(8,128)}, u32[]{:S(2)}) copy-start(f32[1,2,256,256]{3,2,1,0:T(8,128)} %param.12) | copy-start | bytes 1572868
  4.5 1.0 %copy-start.3 = (f32[1,2,256,256]{3,2,1,0:T(8,128)S(1)}, f32[1,2,256,256]{3,2,1,0:T(8,128)}, u32[]{:S(2)}) copy-start(f32[1,2,256,256]{3,2,1,0:T(8,128)} %param.13) | copy-start | bytes 1572868
  5.6 1.0 %copy-start.4 = (f32[1,2,256,256]{3,2,1,0:T(8,128)S(1)}, f32[1,2,256,256]{3,2,1,0:T(8,128)}, u32[]{:S(2)}) copy-start(f32[1,2,256,256]{3,2,1,0:T(8,128)} %param.14) | copy-start | bytes 1572868
  6.6 1.0 %copy-start.5 = (f32[1,2,256,256]{3,2,1,0:T(8,128)S(1)}, f32[1,2,256,256]{3,2,1,0:T(8,128)}, u32[]{:S(2)}) copy-start(f32[1,2,256,256]{3,2,1,0:T(8,128)} %param.15) | copy-start | bytes 1572868
  7.7 0.9 %copy-start.6 = (bf16[256,512]{1,0:T(8,128)(2,1)S(1)}, bf16[256,512]{1,0:T(8,128)(2,1)}, u32[]{:S(2)}) copy-start(bf16[256,512]{1,0:T(8,128)(2,1)} %ctx.1) | copy-start | bytes 786436

commit v2 on v1

v2 whole, which is shorter than its diff:
```python
import functools

import jax
import jax.numpy as jnp
from jax import lax
from jax.experimental import pallas as pl
from jax.experimental.pallas import tpu as pltpu
from jax.sharding import Mesh
from jax.sharding import PartitionSpec as P

MESH = pl.DeviceIdType.MESH
bf16 = jnp.bfloat16
f32 = jnp.float32
decay_rate = 0.95

NZ, NY, NX = 8, 4, 4
TOK = 256
BLOCK = 256
BAND = 512
COLS = 1024
PATCH = BLOCK // NY
QC = COLS // NY
STRIP = BLOCK // NZ
Y_OFF = (0, -1, 1, 2)
PEER_OFF = (1, -1, 2)
REL = (4, 3, -3, 2, -2, 1, -1, 0)
SETS = ((0, 64), (64, 192), (192, 320), (320, 512))
X_OFF = (0, -1, 1, 2)


class Names:
    def __init__(self):
        self.ids = {}

    def __call__(self, *name):
        return self.ids.setdefault(name, len(self.ids))


N_SEND, N_RECV = 160, 128


def kernel(
    ctx_h, cot_h, tbl, inv, ls, rs, rl, rr, sm,
    ln, rn, sn, sd,
    ctx, cot, turn, pieces, bq, aall, cbuf, zr, summed, out1, in1, grad, dirs, in2, rows,
    ls_v, rs_v, rl_v, rr_v, sm_v,
    send_sems, recv_sems, a1s, a1r, a2s, a2r, loc,
):
    x, y, z, c = (lax.axis_index(n) for n in ("x", "y", "z", "c"))
    me = z * NY + y
    t_me = x * 2 + c
    started = []
    sid, rid = Names(), Names()

    def wrap(v, n):
        return lax.rem(v + n, n)

    def send(src, dst, name, **where):
        k = sid(len(started))
        copy = pltpu.make_async_remote_copy(
            src_ref=src, dst_ref=dst,
            send_sem=send_sems.at[k], recv_sem=recv_sems.at[rid(*name)],
            device_id=where, device_id_type=MESH,
        )
        copy.start()
        started.append(copy)

    def arrived(dst, *name):
        pltpu.make_async_remote_copy(
            src_ref=dst, dst_ref=dst,
            send_sem=send_sems.at[0], recv_sem=recv_sems.at[rid(*name)],
            device_id={"c": 1 - c}, device_id_type=MESH,
        ).wait_recv()

    y_at = {off: wrap(y + off, NY) for off in (0, 1, -1, 2)}
    xp, xm = wrap(x + 1, NX), wrap(x - 1, NX)
    zp, zm = wrap(z + 1, NZ), wrap(z - 1, NZ)

    load_cot = pltpu.make_async_copy(cot_h, cot, loc.at[9])
    load_ctx = pltpu.make_async_copy(ctx_h, ctx, loc.at[10])
    load_cot.start()
    load_ctx.start()
    stats = [
        pltpu.make_async_copy(a, b, loc.at[i])
        for i, (a, b) in enumerate(((rl, rl_v), (rr, rr_v), (sm, sm_v), (ls, ls_v), (rs, rs_v)))
    ]

    barrier = pltpu.get_barrier_semaphore()
    near = [{"y": y_at[off]} for off in PEER_OFF] + [{"x": xp}, {"x": xm}, {"z": zp}, {"z": zm}, {"c": 1 - c}]
    for where in near:
        pl.semaphore_signal(barrier, inc=1, device_id=where, device_id_type=MESH)

    src_col = lax.broadcasted_iota(jnp.int32, (512, 512), 0)
    q = lax.broadcasted_iota(jnp.int32, (512, 512), 1)
    lane = lax.rem(q, 128)
    y_of = lax.rem(q // 128 + y, NY)
    pick = (src_col == (lane // PATCH) * BLOCK + PATCH * y_of + lax.rem(lane, PATCH)).astype(f32).astype(bf16)
    load_cot.wait()
    for j in range(2):
        got = jnp.dot(cot[:, 512 * j : 512 * j + 512], pick, preferred_element_type=f32).astype(bf16)
        for r in range(NY):
            pieces[r, :, 128 * j : 128 * j + 128] = got[:, 128 * r : 128 * r + 128]

    def bpart(t, ya, half=None):
        if half is None:
            return bq.at[t, pl.ds(ya * TOK, TOK)]
        return bq.at[t, pl.ds(ya * TOK + half * (TOK // 2), TOK // 2)]

    pl.semaphore_wait(barrier, len(near))

    here = bpart(t_me, y)
    send(pieces.at[1], here, ("By", -1), y=y_at[1])
    send(pieces.at[3], here, ("By", 1), y=y_at[-1])
    send(pieces.at[0], here, ("Bx", -1, 0), x=xp)
    send(pieces.at[0], here, ("Bx", 1, 0), x=xm)
    send(pieces.at[0], here, ("Bc", 0, 0), c=1 - c)
    for copy in stats:
        copy.start()

    load_ctx.wait()
    turn[...] = ctx[...].astype(f32).T.astype(bf16)
    lanes = pl.ds(pl.multiple_of(y * TOK, TOK), TOK)
    for pos, rel in enumerate(REL):
        zz = wrap(z + rel, NZ)
        for h in range(2):
            aall[pos * 64 + h * 32 : pos * 64 + h * 32 + 32, lanes] = turn[
                pl.ds(pl.multiple_of(h * 256 + zz * 32, 32), 32)
            ]

    def apart(off, k):
        first, end = SETS[k]
        return aall.at[pl.ds(first, end - first), pl.ds(pl.multiple_of(y_at[off] * TOK, TOK), TOK)]

    def send_rows(k):
        for off in PEER_OFF:
            send(apart(0, k), apart(0, k), ("A", k, -off if off != 2 else 2), y=y_at[off])

    send_rows(0)
    send(pieces.at[2], here, ("By", 2), y=y_at[2])
    for k in range(1, len(SETS)):
        send_rows(k)
    bq[t_me, pl.ds(y * TOK, TOK)] = pieces[0]

    def spread(yi):
        part = bpart(t_me, y_at[Y_OFF[yi]])
        arrived(part, "By", Y_OFF[yi])
        send(part, part, ("Bx", -1, yi), x=xp)
        send(part, part, ("Bx", 1, yi), x=xm)
        send(part, part, ("Bc", 0, yi), c=1 - c)

    def pass_on(yi):
        ya = y_at[Y_OFF[yi]]
        for off, x_at, half, to in ((-1, xm, 0, xp), (1, xp, 1, xm)):
            t = x_at * 2 + c
            arrived(bpart(t, ya), "Bx", off, yi)
            send(bpart(t, ya, half), bpart(t, ya, half), ("Bx2", half, yi), x=to)
            send(bpart(t, ya), bpart(t, ya), ("Bc", off, yi), c=1 - c)

    def far(yi):
        t = wrap(x + 2, NX) * 2 + c
        ya = y_at[Y_OFF[yi]]
        arrived(bpart(t, ya, 0), "Bx2", 0, yi)
        arrived(bpart(t, ya, 1), "Bx2", 1, yi)
        send(bpart(t, ya), bpart(t, ya), ("Bc", 2, yi), c=1 - c)

    def rows_here(k):
        for off in PEER_OFF:
            arrived(apart(off, k), "A", k, off)

    def columns_here(u):
        if u % 2:
            for yi in range(NY):
                arrived(here, "Bc", X_OFF[u // 2], yi)

    def piece_of(u):
        xa = wrap(x + X_OFF[u // 2], NX)
        return xa * 2 + (1 - c if u % 2 else c)

    def product(u, k, end=None):
        first = SETS[k][0]
        last_row = SETS[k if end is None else end][1]
        total = jnp.dot(aall[first:last_row], bq[piece_of(u)], preferred_element_type=f32)
        cbuf[u, first // 64 : last_row // 64] = total.astype(bf16).reshape((last_row - first) // 64, 64, QC)

    def step(u, s):
        for d, to in ((0, zp), (1, zm)):
            name = ("Z", u, d, s)
            half = pl.ds(32 * d, 32)
            if s == 1:
                send(cbuf.at[u, 0, half], zr.at[u, d, 0, half], name, z=to)
                continue
            pos = 2 * s - 3 + d
            if s == 2:
                arrived(zr.at[u, d, 0, half], "Z", u, d, 1)
                cbuf[u, pos, half] = (cbuf[u, pos, half].astype(f32) + zr[u, d, 0, half].astype(f32)).astype(bf16)
            else:
                arrived(zr.at[u, d, s - 2], "Z", u, d, s - 1)
                cbuf[u, pos] = (cbuf[u, pos].astype(f32) + zr[u, d, s - 2].astype(f32)).astype(bf16)
            send(cbuf.at[u, pos], zr.at[u, d, s - 1], name, z=to)

    def last(u):
        arrived(zr.at[u, 0, 3], "Z", u, 0, 4)
        arrived(zr.at[u, 1, 3], "Z", u, 1, 4)
        whole = cbuf[u, 7].astype(f32) + zr[u, 0, 3].astype(f32) + zr[u, 1, 3].astype(f32)
        for j in range(2):
            tile = whole[:, 128 * j : 128 * j + 128]
            summed[piece_of(u) * 2 + j, 0] = tile[:32]
            summed[piece_of(u) * 2 + j, 1] = tile[32:]

    def steps(*pairs):
        for u, s in pairs:
            step(u, s)

    spread(1)
    spread(2)
    pass_on(0)
    rows_here(0)
    spread(3)
    product(0, 0)
    step(0, 1)
    columns_here(1)
    product(1, 0)
    step(1, 1)
    pass_on(1)
    pass_on(2)
    rows_here(1)
    for u in (0, 1):
        product(u, 1)
        step(u, 2)
    rows_here(2)
    for u in (0, 1):
        product(u, 2)
        step(u, 3)
    pass_on(3)
    for u in (2, 4, 3, 5):
        columns_here(u)
        product(u, 0, 2)
        step(u, 1)
    rows_here(3)
    for u in (0, 1):
        product(u, 3)
        step(u, 4)
    for yi in range(NY - 1):
        far(yi)
    for u in (2, 4, 3, 5):
        product(u, 3)
        step(u, 2)
    far(3)
    for u in (6, 7):
        columns_here(u)
        product(u, 0, 3)
        step(u, 1)
    steps((2, 3), (4, 3), (3, 3), (5, 3))
    last(0)
    last(1)
    steps((6, 2), (7, 2), (2, 4), (4, 4), (6, 3), (7, 3), (3, 4), (5, 4), (6, 4), (7, 4))
    for u in (2, 4, 3, 5, 6, 7):
        last(u)

    left_lanes = lax.broadcasted_iota(jnp.int32, (16, 128), 1) < 64

    def patch(f, s):
        k = tbl[0, 2 * f + s]
        col = k & 31
        tile = summed[col >> 1, k >> 5]
        odd = (col & 1) == 1
        upper, lower = tile[:16], tile[16:]
        first = jnp.where(odd, pltpu.roll(upper, 64, 1), upper)
        second = jnp.where(odd, lower, pltpu.roll(lower, 64, 1))
        return jnp.where(left_lanes, first, second).astype(bf16)

    def other(i):
        k = i // NY
        dz = 4 + ((k + 1) // 2) * (1 - 2 * lax.rem(k, 2))
        zd = lax.rem(z + dz, NZ)
        yd = lax.rem(y + 3 - lax.rem(i, NY), NY)
        return zd, yd, zd * NY + yd

    def copy1(i, s):
        zd, yd, f = other(i)
        return pltpu.make_async_remote_copy(
            src_ref=out1.at[s, i], dst_ref=in1.at[s, me], send_sem=a1s.at[s, i], recv_sem=a1r.at[s, i],
            device_id={"z": zd, "y": yd}, device_id_type=MESH,
        )

    def copy2(i, s):
        zd, yd, f = other(i)
        return pltpu.make_async_remote_copy(
            src_ref=dirs.at[s, lax.rem(f, 16)], dst_ref=in2.at[s, me], send_sem=a2s.at[s, i], recv_sem=a2r.at[s, i],
            device_id={"z": zd, "y": yd}, device_id_type=MESH,
        )

    def each(do):
        def body(i, carry):
            do(i)
            return carry

        lax.fori_loop(0, 31, body, 0)

    for s in range(2):

        def send1(i, s=s):
            f = other(i)[2]
            out1[s, i] = patch(f, s)
            copy1(i, s).start()

        each(send1)
        in1[s, me] = patch(me, s)

    highest = lax.Precision.HIGHEST
    for copy in stats[:3]:
        copy.wait()
    out_sn = []
    for s in range(2):
        each(lambda i, s=s: copy1(i, s).wait_recv())
        for j in range(2):
            for zz in range(NZ):
                a = in1[s, zz * NY + 2 * j].astype(f32)
                b = in1[s, zz * NY + 2 * j + 1].astype(f32)
                at = pl.ds(128 * j, 128)
                grad[s, 32 * zz : 32 * zz + 16, at] = jnp.where(left_lanes, a, pltpu.roll(b, 64, 1))
                grad[s, 32 * zz + 16 : 32 * zz + 32, at] = jnp.where(left_lanes, pltpu.roll(a, 64, 1), b)
        g = grad[s]
        second = decay_rate * sm_v[s] + (1.0 - decay_rate) * g * g
        sm_v[s] = second
        adam = g / (jnp.sqrt(second) + 1e-08)
        shaped = jnp.dot(rl_v[s], g, precision=highest, preferred_element_type=f32)
        shaped = jnp.dot(shaped, rr_v[s], precision=highest, preferred_element_type=f32)
        ratio = jnp.sqrt(jnp.sum(adam * adam, keepdims=True)) / jnp.sqrt(
            jnp.sum(shaped * shaped, keepdims=True) + 1e-06
        )
        dirs[s] = (shaped * ratio).astype(bf16).reshape(16, 16, BLOCK)
        each(lambda i, s=s: copy2(i, s).start())
        in2[s, me] = dirs[s, lax.rem(me, 16)]

    out_sn = pltpu.make_async_copy(sm_v, sn, loc.at[5])
    out_sn.start()
    for copy in stats[3:]:
        copy.wait()
    for s in range(2):
        g = grad[s].astype(bf16)
        left = lax.dot_general(g, g, (((1,), (1,)), ((), ())), preferred_element_type=f32)
        ls_v[s] = decay_rate * ls_v[s] + (1.0 - decay_rate) * left / BLOCK
        right = lax.dot_general(g, g, (((0,), (0,)), ((), ())), preferred_element_type=f32)
        rs_v[s] = decay_rate * rs_v[s] + (1.0 - decay_rate) * right / BLOCK
    out_ln = pltpu.make_async_copy(ls_v, ln, loc.at[6])
    out_rn = pltpu.make_async_copy(rs_v, rn, loc.at[7])
    out_ln.start()
    out_rn.start()

    for copy in started:
        copy.wait_send()
    for s in range(2):
        each(lambda i, s=s: copy1(i, s).wait_send())
    for s in range(2):
        each(lambda i, s=s: copy2(i, s).wait_recv())
    half = me // 16
    for col in range(32):
        p = inv[0, half * 32 + col]
        rows[:, BLOCK * col : BLOCK * col + BLOCK] = in2[p & 1, p >> 1]
    out_sd = pltpu.make_async_copy(rows, sd, loc.at[8])
    out_sd.start()
    for s in range(2):
        each(lambda i, s=s: copy2(i, s).wait_send())
    for copy in (out_sn, out_ln, out_rn, out_sd):
        copy.wait()


def per_device(context, cotangent, block_table, left_stat, right_stat, root_left, root_right, second_moment):
    ids = jnp.arange(64, dtype=jnp.int32)
    inverse = jnp.sum(jnp.where(block_table[0][None, :] == ids[:, None], ids[None, :], 0), axis=1)[None]
    smem = pl.BlockSpec(memory_space=pltpu.SMEM)
    hbm = pl.BlockSpec(memory_space=pltpu.HBM)
    block = jax.ShapeDtypeStruct((2, BLOCK, BLOCK), f32)
    V = pltpu.VMEM
    DMA = pltpu.SemaphoreType.DMA
    ln, rn, sn, sd = pl.pallas_call(
        kernel,
        out_shape=(block, block, block, jax.ShapeDtypeStruct((16, 8192), bf16)),
        in_specs=[hbm, hbm, smem, smem, hbm, hbm, hbm, hbm, hbm],
        out_specs=(hbm, hbm, hbm, hbm),
        scratch_shapes=[
            V((TOK, BAND), bf16),
            V((TOK, COLS), bf16),
            V((BAND, TOK), bf16),
            V((NY, TOK, QC), bf16),
            V((8, NY * TOK, QC), bf16),
            V((BAND, NY * TOK), bf16),
            V((8, NZ, 64, QC), bf16),
            V((8, 2, 4, 64, QC), bf16),
            V((16, 2, 32, 128), f32),
            V((2, 32, 16, 128), bf16),
            V((2, 32, 16, 128), bf16),
            V((2, BLOCK, BLOCK), f32),
            V((2, 16, 16, BLOCK), bf16),
            V((2, 32, 16, BLOCK), bf16),
            V((16, 8192), bf16),
            *[V((2, BLOCK, BLOCK), f32)] * 5,
            DMA((N_SEND,)),
            DMA((N_RECV,)),
            DMA((2, 32)),
            DMA((2, 32)),
            DMA((2, 32)),
            DMA((2, 32)),
            DMA((11,)),
        ],
        compiler_params=pltpu.CompilerParams(collective_id=0, has_side_effects=True, vmem_limit_bytes=67_043_328),
        name="shampoo",
    )(
        context, cotangent, block_table, inverse,
        left_stat[0], right_stat[0], root_left[0], root_right[0], second_moment[0],
    )
    return ln[None], rn[None], sn[None], sd[None]


def solution(mesh):
    finer = Mesh(mesh.devices.reshape(NZ, NY, NX, 2), ("z", "y", "x", "c"))
    F, T = ("z", "y"), ("x", "c")
    stat = P(T, F, None, None)
    return jax.shard_map(
        per_device,
        mesh=finer,
        in_specs=(P(F, T), P(F, T), P(T, None), stat, stat, stat, stat, stat),
        out_specs=(stat, stat, stat, P(T, F, None)),
        check_vma=False,
    )
```

time: 96 us -> 82.9 us (0.86)
  Pallas kernels: 83.2 us -> 75.7 us
  local copies, waits for them, and re-layouts: 10.9 us -> 5.6 us
    pallas_call x1, Pallas kernels: 83.2 us -> 75.7 us  [per_device(): pl.pallas_call(kernel, out_shape=(block, block, block, jax.ShapeDtypeStru...]
    unnamed x20 -> x12, local copies, waits for them, and re-layouts: 10.9 us -> 5.6 us
where the time goes in v2:
time: 82.9 us; the launch traced here: 82.6 us
  Pallas kernels  75.7 us (91%)
  local copies, waits for them, and re-layouts  5.6 us (7%)
    pallas_call x1, Pallas kernels, per_device(): pl.pallas_call(kernel, out_shape=(block, block, block, jax.ShapeDtypeStru...  75.7 us
    unnamed x12, local copies, waits for them, and re-layouts  5.6 us

profile of v2, /device:TPU:32, one launch (start us, length us, event | category | flops | bytes accessed | tf_op | source)
XLA Modules:
  0.0 82.6 jit_solution(11953737883314989643)
XLA Ops:
  0.6 0.0 copy-start.3
  0.6 0.6 copy-done.3
  1.3 0.6 select_reduce_fusion
  1.9 75.7 %shampoo.1 = (f32[2,256,256]{2,1,0:T(8,128)}, f32[2,256,256]{2,1,0:T(8,128)}, f32[2,256,256]{2,1,0:T(8,128)}, bf16[16,8192]{1,0:T(8,128)(2,1)}) custom-call(bf16[256,512]{1,0:T(8,128)(2,1)} %ctx_h.1, bf16[256,1024]{1,0:T(8,128)(2,1)} %cot_h.1, s32[1,64]{1,0:T(1,128)} %tbl.1, s32[1,64]{1,0:T(1,128)} %bitcast.21, f32[2,256,256]{2,1,0:T(8,128)} %bitcast.11, ...), custom_call_target="tpu_custom_call" | custom-call | tf_op jit(solution)/shard_map/shampoo/pallas_call | solution.py:377
  77.7 0.0 copy-start.1
  77.7 1.9 %copy.16 = f32[1,2,256,256]{3,2,1,0:T(8,128)} copy(f32[1,2,256,256]{3,2,1,0:T(8,128)} %bitcast.18) | data formatting | bytes 1048576
  79.6 0.0 copy-done.1
  79.6 0.0 copy-start
  79.6 0.8 copy.17
  80.4 0.4 copy-done
  80.8 0.0 copy-start.2
  80.8 0.8 copy.18
  81.6 0.3 copy-done.2
  81.9 0.7 copy.19
Async XLA Ops:
  0.6 0.7 copy-start.3
  77.7 1.9 %copy-start.1 = (f32[2,256,256]{2,1,0:T(8,128)S(1)}, f32[2,256,256]{2,1,0:T(8,128)}, u32[]{:S(2)}) copy-start(f32[2,256,256]{2,1,0:T(8,128)} %get-tuple-element.9) | copy-start | bytes 1572868
  79.6 1.2 %copy-start = (f32[2,256,256]{2,1,0:T(8,128)S(1)}, f32[2,256,256]{2,1,0:T(8,128)}, u32[]{:S(2)}) copy-start(f32[2,256,256]{2,1,0:T(8,128)} %get-tuple-element.10) | copy-start | bytes 1572868
  80.8 1.1 %copy-start.2 = (bf16[16,8192]{1,0:T(8,128)(2,1)S(1)}, bf16[16,8192]{1,0:T(8,128)(2,1)}, u32[]{:S(2)}) copy-start(bf16[16,8192]{1,0:T(8,128)(2,1)} %get-tuple-element.11) | copy-start | bytes 786436

commit v3 on v2

v3 whole, which is shorter than its diff:
```python
import functools

import jax
import jax.numpy as jnp
from jax import lax
from jax.experimental import pallas as pl
from jax.experimental.pallas import tpu as pltpu
from jax.sharding import Mesh
from jax.sharding import PartitionSpec as P

MESH = pl.DeviceIdType.MESH
bf16 = jnp.bfloat16
f32 = jnp.float32
decay_rate = 0.95

NZ, NY, NX = 8, 4, 4
TOK = 256
BLOCK = 256
BAND = 512
COLS = 1024
PATCH = BLOCK // NY
QC = COLS // NY
STRIP = BLOCK // NZ
Y_OFF = (0, -1, 1, 2)
PEER_OFF = (1, -1, 2)
REL = (4, 3, -3, 2, -2, 1, -1, 0)
SETS = ((0, 64), (64, 192), (192, 320), (320, 512))
X_OFF = (0, -1, 1, 2)

PLAN = (
    ("first",), ("xd", 0, 0), ("turn",), ("yq", "A", 0), ("yq", "B2", 0), ("yq", "A", 1), ("yq", "A", 2),
    ("yq", "A", 3), ("sp", 1, 0), ("sp", 2, 0), ("got", 0, 0, -1), ("got", 0, 0, 1), ("sp", 3, 0),
    ("pr", 0, 0, 0, 0), ("z", 0, 0, 1, 0), ("z", 0, 0, 1, 1), ("pr", 1, 0, 0, 0), ("z", 1, 0, 1, 0),
    ("z", 1, 0, 1, 1), ("got", 1, 0, -1), ("got", 1, 0, 1), ("rel", 1, 0, 0), ("rel", 1, 0, 1), ("far", 0, 0),
    ("pr", 0, 0, 1, 1), ("z", 0, 0, 2, 0), ("z", 0, 0, 2, 1), ("pr", 1, 0, 1, 1), ("z", 1, 0, 2, 0),
    ("z", 1, 0, 2, 1), ("got", 2, 0, -1), ("got", 2, 0, 1), ("rel", 2, 0, 0), ("rel", 2, 0, 1), ("pr", 0, 0, 2, 2),
    ("z", 0, 0, 3, 0), ("z", 0, 0, 3, 1), ("pr", 1, 0, 2, 2), ("z", 1, 0, 3, 0), ("z", 1, 0, 3, 1),
    ("got", 3, 0, -1), ("got", 3, 0, 1), ("rel", 3, 0, 0), ("rel", 3, 0, 1), ("pr", 2, 0, 0, 2), ("z", 2, 0, 1, 0),
    ("z", 2, 0, 1, 1), ("pr", 4, 0, 0, 2), ("z", 4, 0, 1, 0), ("z", 4, 0, 1, 1), ("far", 1, 0), ("pr", 3, 0, 0, 2),
    ("z", 3, 0, 1, 0), ("z", 3, 0, 1, 1), ("pr", 5, 0, 0, 2), ("z", 5, 0, 1, 0), ("z", 5, 0, 1, 1),
    ("pr", 0, 0, 3, 3), ("z", 0, 0, 4, 0), ("z", 0, 0, 4, 1), ("pr", 1, 0, 3, 3), ("z", 1, 0, 4, 0),
    ("z", 1, 0, 4, 1), ("far", 2, 0), ("z", 2, 0, 2, 0), ("z", 2, 0, 2, 1), ("z", 4, 0, 2, 0), ("z", 4, 0, 2, 1),
    ("far", 3, 0), ("z", 3, 0, 2, 0), ("z", 3, 0, 2, 1), ("z", 5, 0, 2, 0), ("z", 5, 0, 2, 1), ("pr", 6, 0, 0, 3),
    ("z", 6, 0, 1, 0), ("z", 6, 0, 1, 1), ("pr", 7, 0, 0, 3), ("z", 7, 0, 1, 0), ("z", 7, 0, 1, 1),
    ("pr", 2, 0, 3, 3), ("z", 2, 0, 3, 0), ("z", 2, 0, 3, 1), ("pr", 4, 0, 3, 3), ("z", 4, 0, 3, 0),
    ("z", 4, 0, 3, 1), ("pr", 3, 0, 3, 3), ("z", 3, 0, 3, 0), ("z", 3, 0, 3, 1), ("pr", 5, 0, 3, 3),
    ("z", 5, 0, 3, 0), ("z", 5, 0, 3, 1), ("last", 0, 0), ("last", 1, 0), ("z", 6, 0, 2, 0), ("z", 6, 0, 2, 1),
    ("z", 7, 0, 2, 0), ("z", 7, 0, 2, 1), ("z", 2, 0, 4, 0), ("z", 2, 0, 4, 1), ("z", 4, 0, 4, 0), ("z", 4, 0, 4, 1),
    ("z", 6, 0, 3, 0), ("z", 6, 0, 3, 1), ("z", 7, 0, 3, 0), ("z", 7, 0, 3, 1), ("z", 3, 0, 4, 0), ("z", 3, 0, 4, 1),
    ("z", 5, 0, 4, 0), ("z", 5, 0, 4, 1), ("z", 6, 0, 4, 0), ("z", 6, 0, 4, 1), ("z", 7, 0, 4, 0), ("z", 7, 0, 4, 1),
    ("last", 2, 0), ("last", 4, 0), ("last", 3, 0), ("last", 5, 0), ("last", 6, 0), ("last", 7, 0),
)


class Names:

    def __init__(self):
        self.ids = {}

    def __call__(self, *name):
        return self.ids.setdefault(name, len(self.ids))


N_SEND = N_RECV = 320
PARTS = 1
HALF = QC // PARTS
STRAIGHT = (0,)
TWO = ()


def kernel(
    ctx_h, cot_h, tbl, ls, rs, rl, rr, sm,
    ln, rn, sn, in2,
    ctx, cot, turn, pieces, bq, aall, cbuf, zr, summed, out1, in1, grad, dirs,
    ls_v, rs_v, rl_v, rr_v, sm_v,
    send_sems, recv_sems, a1s, a1r, a2s, a2r, loc,
):
    x, y, z, c = (lax.axis_index(n) for n in ("x", "y", "z", "c"))
    me = z * NY + y
    t_me = x * 2 + c
    started = []
    waited = set()
    rid = Names()

    def wrap(v, n):
        return lax.rem(v + n, n)

    def send(src, dst, name, **where):
        copy = pltpu.make_async_remote_copy(
            src_ref=src, dst_ref=dst,
            send_sem=send_sems.at[len(started)], recv_sem=recv_sems.at[rid(*name)],
            device_id=where, device_id_type=MESH,
        )
        copy.start()
        started.append(copy)

    def need(dst, *name):
        if name in waited:
            return
        waited.add(name)
        pltpu.make_async_remote_copy(
            src_ref=dst, dst_ref=dst,
            send_sem=send_sems.at[0], recv_sem=recv_sems.at[rid(*name)],
            device_id={"c": 1 - c}, device_id_type=MESH,
        ).wait_recv()

    y_at = {off: wrap(y + off, NY) for off in (0, 1, -1, 2)}
    x_at = {off: wrap(x + off, NX) for off in (0, 1, -1, 2)}
    z_to = (wrap(z + 1, NZ), wrap(z - 1, NZ))
    z_two = (wrap(z + 2, NZ), wrap(z - 2, NZ))

    load_cot = pltpu.make_async_copy(cot_h, cot, loc.at[8])
    load_ctx = pltpu.make_async_copy(ctx_h, ctx, loc.at[9])
    load_cot.start()
    load_ctx.start()
    stats = [
        pltpu.make_async_copy(a, b, loc.at[i])
        for i, (a, b) in enumerate(((rl, rl_v), (rr, rr_v), (sm, sm_v), (ls, ls_v), (rs, rs_v)))
    ]

    barrier = pltpu.get_barrier_semaphore()
    near = [{"x": x_at[2]}] + [{"z": v} for v in z_two] + [{"y": y_at[off]} for off in PEER_OFF] + [{"x": x_at[1]}, {"x": x_at[-1]}]
    near += [{"z": z_to[0]}, {"z": z_to[1]}, {"c": 1 - c}]
    for where in near:
        pl.semaphore_signal(barrier, inc=1, device_id=where, device_id_type=MESH)

    src_col = lax.broadcasted_iota(jnp.int32, (512, 512), 0)
    q = lax.broadcasted_iota(jnp.int32, (1, 512), 1)
    from_col = (((q & 127) >> 6) << 8) + ((((q >> 7) + y) & 3) << 6) + (q & 63)
    pick = (src_col == from_col).astype(f32).astype(bf16)
    load_cot.wait()
    for j in range(2):
        got = jnp.dot(cot[:, 512 * j : 512 * j + 512], pick, preferred_element_type=f32).astype(bf16)
        for r in range(NY):
            at = pl.ds(j % (2 // PARTS) * 128, 128)
            pieces[r, j * PARTS // 2, :, at] = got[:, 128 * r : 128 * r + 128]

    def bpart(t, j, ya, half=None):
        if half is None:
            return bq.at[t, j, pl.ds(ya * TOK, TOK)]
        return bq.at[t, j, pl.ds(ya * TOK + half * (TOK // 2), TOK // 2)]

    def apart(off, k, half=None):
        first, end = SETS[k]
        size = end - first
        if half is not None:
            size //= 2
            first += half * size
        return aall.at[pl.ds(first, size), pl.ds(pl.multiple_of(y_at[off] * TOK, TOK), TOK)]

    def send_by(j):
        send(pieces.at[1, j], bpart(t_me, j, y), ("By", -1, j), y=y_at[1])
        send(pieces.at[3, j], bpart(t_me, j, y), ("By", 1, j), y=y_at[-1])

    def send_pieces(src, part, yi, j):
        send(src, part, ("Bx", -1, yi, j), x=x_at[1])
        send(src, part, ("Bx", 1, yi, j), x=x_at[-1])
        send(src, part, ("Bc", 0, yi, j), c=1 - c)

    def first():
        send_by(0)
        for j in range(PARTS):
            send_pieces(pieces.at[0, j], bpart(t_me, j, y), 0, j)
        for copy in stats:
            copy.start()

    def turned():
        load_ctx.wait()
        turn[...] = ctx[...].astype(f32).T.astype(bf16)
        lanes = pl.ds(pl.multiple_of(y * TOK, TOK), TOK)
        for pos, rel in enumerate(REL):
            zz = wrap(z + rel, NZ)
            for h in range(2):
                aall[pos * 64 + h * 32 : pos * 64 + h * 32 + 32, lanes] = turn[
                    pl.ds(pl.multiple_of(h * 256 + zz * 32, 32), 32)
                ]
        for j in range(PARTS):
            bq[t_me, j, pl.ds(y * TOK, TOK)] = pieces[0, j]

    def over_y(what, k):
        if what == "A":
            send(apart(0, k), apart(0, k), ("A", k, -1), y=y_at[1])
            send(apart(0, k), apart(0, k), ("A", k, 1), y=y_at[-1])
            send(apart(0, k), apart(0, k), ("A", k, 2), y=y_at[2])
        elif what == "By":
            send_by(k)
        else:
            send(pieces.at[2, k], bpart(t_me, k, y), ("By", 2, k), y=y_at[2])

    def pass_rows(k, h):
        off = 2 * h - 1
        need(apart(off, k), "A", k, off)
        send(apart(off, k, h), apart(off, k, h), ("A2", k, h), y=y_at[-off])

    def from_y(yi, j):
        need(bpart(t_me, j, y_at[Y_OFF[yi]]), "By", Y_OFF[yi], j)

    def spread(yi, j):
        from_y(yi, j)
        part = bpart(t_me, j, y_at[Y_OFF[yi]])
        send_pieces(part, part, yi, j)

    def x_part(off, yi, j, half=None):
        return bpart(x_at[off] * 2 + c, j, y_at[Y_OFF[yi]], half)

    def from_x(off, yi, j):
        if off == 2:
            if yi in STRAIGHT:
                need(x_part(2, yi, j), "Bx2", 0, yi, j)
                return
            for h in range(2):
                need(x_part(2, yi, j, h), "Bx2", h, yi, j)
        else:
            need(x_part(off, yi, j), "Bx", off, yi, j)

    def share(yi, j, off):
        from_x(off, yi, j)
        send(x_part(off, yi, j), x_part(off, yi, j), ("Bc", off, yi, j), c=1 - c)

    def relay(yi, j, h):
        off = 2 * h - 1
        from_x(off, yi, j)
        send(x_part(off, yi, j, h), x_part(off, yi, j, h), ("Bx2", h, yi, j), x=x_at[-off])

    def straight(yi, j):
        if yi:
            from_y(yi, j)
        src = bpart(t_me, j, y_at[Y_OFF[yi]]) if yi else pieces.at[0, j]
        send(src, bpart(t_me, j, y_at[Y_OFF[yi]]), ("Bx2", 0, yi, j), x=x_at[2])

    def piece_of(u):
        return x_at[X_OFF[u // 2]] * 2 + (1 - c if u % 2 else c)

    def product(u, j, k, end):
        off = X_OFF[u // 2]
        for yi in range(NY):
            if u % 2:
                need(bpart(t_me, j, y), "Bc", off, yi, j)
            elif off:
                from_x(off, yi, j)
            elif yi:
                from_y(yi, j)
        for kk in range(k, end + 1):
            for off in (-1, 1):
                need(apart(off, kk), "A", kk, off)
            need(apart(2, kk), "A", kk, 2)
        r0, r1 = SETS[k][0], SETS[end][1]
        total = jnp.dot(aall[r0:r1], bq[piece_of(u), j], preferred_element_type=f32)
        cbuf[u, j, r0 // 64 : r1 // 64] = total.astype(bf16).reshape((r1 - r0) // 64, 64, HALF)

    def step(u, j, s, d):
        name = ("Z", u, j, d, s)
        half = pl.ds(32 * d, 32)
        if s == 1:
            send(cbuf.at[u, j, 0, half], zr.at[u, j, d, 0, half], name, z=z_to[d])
            return
        pos = 2 * s - 3 + d
        if s == 2:
            need(zr.at[u, j, d, 0, half], "Z", u, j, d, 1)
            cbuf[u, j, pos, half] = (
                cbuf[u, j, pos, half].astype(f32) + zr[u, j, d, 0, half].astype(f32)
            ).astype(bf16)
        else:
            need(zr.at[u, j, d, s - 2], "Z", u, j, d, s - 1)
            cbuf[u, j, pos] = (cbuf[u, j, pos].astype(f32) + zr[u, j, d, s - 2].astype(f32)).astype(bf16)
        send(cbuf.at[u, j, pos], zr.at[u, j, d, s - 1], name, z=z_to[d])

    def two_start(u, j):
        for d in range(2):
            half = pl.ds(32 * d, 32)
            send(cbuf.at[u, j, 0, half], zr.at[u, j, d, 0, half], ("Z", u, j, d, 1), z=z_two[d])
            send(cbuf.at[u, j, 1 + d], zr.at[u, j, d, 1], ("Z", u, j, d, 2), z=z_to[d])

    def two_near(u, j):
        for d in range(2):
            send(cbuf.at[u, j, 5 + d], zr.at[u, j, d, 3], ("Z", u, j, d, 4), z=z_to[d])

    def two_end(u, j):
        for d in range(2):
            half = pl.ds(32 * d, 32)
            need(zr.at[u, j, d, 0, half], "Z", u, j, d, 1)
            need(zr.at[u, j, d, 1], "Z", u, j, d, 2)
            for h in range(2):
                at = pl.ds(32 * h, 32)
                part = cbuf[u, j, 3 + d, at].astype(f32) + zr[u, j, d, 1, at].astype(f32)
                if h == d:
                    part += zr[u, j, d, 0, at].astype(f32)
                cbuf[u, j, 3 + d, at] = part.astype(bf16)
            send(cbuf.at[u, j, 3 + d], zr.at[u, j, d, 2], ("Z", u, j, d, 3), z=z_two[d])

    def last(u, j):
        whole = cbuf[u, j, 7].astype(f32)
        for d in range(2):
            need(zr.at[u, j, d, 3], "Z", u, j, d, 4)
            whole += zr[u, j, d, 3].astype(f32)
            if u in TWO:
                need(zr.at[u, j, d, 2], "Z", u, j, d, 3)
                whole += zr[u, j, d, 2].astype(f32)
        for i in range(2 // PARTS):
            tile = whole[:, 128 * i : 128 * i + 128]
            summed[piece_of(u) * 2 + j + i, 0] = tile[:32]
            summed[piece_of(u) * 2 + j + i, 1] = tile[32:]

    pl.semaphore_wait(barrier, len(near))
    acts = {
        "first": first, "turn": turned, "yq": over_y, "rr": pass_rows, "sp": spread, "got": share, "rel": relay, "xd": straight,
        "far": lambda yi, j: share(yi, j, 2), "pr": product, "z": step, "last": last,
        "za": two_start, "zb": two_end, "zc": two_near,
    }
    for act, *rest in PLAN:
        acts[act](*rest)

    left_lanes = lax.broadcasted_iota(jnp.int32, (16, 128), 1) < 64

    def patch(f, s):
        k = tbl[0, 2 * f + s]
        col = k & 31
        tile = summed[col >> 1, k >> 5]
        odd = (col & 1) == 1
        upper, lower = tile[:16], tile[16:]
        first = jnp.where(odd, pltpu.roll(upper, 64, 1), upper)
        second = jnp.where(odd, lower, pltpu.roll(lower, 64, 1))
        return jnp.where(left_lanes, first, second).astype(bf16)

    def other(i):
        k = i // NY
        dz = 4 + ((k + 1) // 2) * (1 - 2 * lax.rem(k, 2))
        zd = lax.rem(z + dz, NZ)
        yd = lax.rem(y + 3 - lax.rem(i, NY), NY)
        return zd, yd, zd * NY + yd

    def copy1(i, s):
        zd, yd, f = other(i)
        return pltpu.make_async_remote_copy(
            src_ref=out1.at[s, i], dst_ref=in1.at[s, me], send_sem=a1s.at[s, i], recv_sem=a1r.at[s, i],
            device_id={"z": zd, "y": yd}, device_id_type=MESH,
        )

    def copy2(i, s):
        zd, yd, f = other(i)
        return pltpu.make_async_remote_copy(
            src_ref=dirs.at[s, lax.rem(f, 16)], dst_ref=in2.at[s, me], send_sem=a2s.at[s, i], recv_sem=a2r.at[s, i],
            device_id={"z": zd, "y": yd}, device_id_type=MESH,
        )

    def each(do):
        def body(k, carry):
            for i in range(NY):
                do(k * NY + i)
            return carry

        lax.fori_loop(0, NZ - 1, body, 0)
        for i in range(NY * (NZ - 1), NY * NZ - 1):
            do(i)

    for s in range(2):

        def send1(k, carry, s=s, dests=NY):
            for i in range(dests):
                out1[s, k * NY + i] = patch(other(k * NY + i)[2], s)
            for i in range(dests):
                copy1(k * NY + i, s).start()
            return carry

        lax.fori_loop(0, NZ - 1, send1, 0)
        send1(NZ - 1, 0, dests=NY - 1)
        in1[s, me] = patch(me, s)

    highest = lax.Precision.HIGHEST
    for copy in stats[:3]:
        copy.wait()
    own = [pltpu.make_async_copy(dirs.at[s, lax.rem(me, 16)], in2.at[s, me], loc.at[10 + s]) for s in range(2)]
    for s in range(2):
        each(lambda i, s=s: copy1(i, s).wait_recv())
        for j in range(2):
            for zz in range(NZ):
                a = in1[s, zz * NY + 2 * j].astype(f32)
                b = in1[s, zz * NY + 2 * j + 1].astype(f32)
                at = pl.ds(128 * j, 128)
                grad[s, 32 * zz : 32 * zz + 16, at] = jnp.where(left_lanes, a, pltpu.roll(b, 64, 1))
                grad[s, 32 * zz + 16 : 32 * zz + 32, at] = jnp.where(left_lanes, pltpu.roll(a, 64, 1), b)
        g = grad[s]
        second = decay_rate * sm_v[s] + (1.0 - decay_rate) * g * g
        sm_v[s] = second
        adam = g / (jnp.sqrt(second) + 1e-08)
        shaped = jnp.dot(rl_v[s], g, precision=highest, preferred_element_type=f32)
        shaped = jnp.dot(shaped, rr_v[s], precision=highest, preferred_element_type=f32)
        ratio = jnp.sqrt(jnp.sum(adam * adam, keepdims=True)) / jnp.sqrt(
            jnp.sum(shaped * shaped, keepdims=True) + 1e-06
        )
        dirs[s] = (shaped * ratio).astype(bf16).reshape(16, 16, BLOCK)
        each(lambda i, s=s: copy2(i, s).start())
        own[s].start()

    out_sn = pltpu.make_async_copy(sm_v, sn, loc.at[5])
    out_sn.start()
    for copy in stats[3:]:
        copy.wait()
    for s in range(2):
        g = grad[s].astype(bf16)
        left = lax.dot_general(g, g, (((1,), (1,)), ((), ())), preferred_element_type=f32)
        ls_v[s] = decay_rate * ls_v[s] + (1.0 - decay_rate) * left / BLOCK
        right = lax.dot_general(g, g, (((0,), (0,)), ((), ())), preferred_element_type=f32)
        rs_v[s] = decay_rate * rs_v[s] + (1.0 - decay_rate) * right / BLOCK
    out_ln = pltpu.make_async_copy(ls_v, ln, loc.at[6])
    out_rn = pltpu.make_async_copy(rs_v, rn, loc.at[7])
    out_ln.start()
    out_rn.start()

    for copy in started:
        copy.wait_send()
    for s in range(2):
        each(lambda i, s=s: copy1(i, s).wait_send())
    for s in range(2):
        each(lambda i, s=s: copy2(i, s).wait_recv())
    for s in range(2):
        each(lambda i, s=s: copy2(i, s).wait_send())
    for copy in (out_sn, out_ln, out_rn, *own):
        copy.wait()


def emit(tbl, ln_i, rn_i, sn_i, in2, ln, rn, sn, sd, ln_v, rn_v, sn_v, strips, rows, inv, sems):
    half = (lax.axis_index("z") * NY + lax.axis_index("y")) // 16
    load = pltpu.make_async_copy(in2, strips, sems.at[3])
    load.start()
    whole = ((ln_i, ln_v, ln), (rn_i, rn_v, rn), (sn_i, sn_v, sn))
    for i, (a, b, _) in enumerate(whole):
        pltpu.make_async_copy(a, b, sems.at[i]).start()
    for p in range(64):
        inv[tbl[0, p]] = p
    load.wait()
    for col in range(32):
        p = inv[half * 32 + col]
        rows[:, BLOCK * col : BLOCK * col + BLOCK] = strips[p & 1, p >> 1]
    last = pltpu.make_async_copy(rows, sd, sems.at[3])
    last.start()
    for i, (a, b, o) in enumerate(whole):
        pltpu.make_async_copy(a, b, sems.at[i]).wait()
        pltpu.make_async_copy(b, o, sems.at[i]).start()
    for i, (a, b, o) in enumerate(whole):
        pltpu.make_async_copy(b, o, sems.at[i]).wait()
    last.wait()


def per_device(context, cotangent, block_table, left_stat, right_stat, root_left, root_right, second_moment):
    smem = pl.BlockSpec(memory_space=pltpu.SMEM)
    hbm = pl.BlockSpec(memory_space=pl.ANY)
    block = jax.ShapeDtypeStruct((2, BLOCK, BLOCK), f32)
    V = pltpu.VMEM
    DMA = pltpu.SemaphoreType.DMA
    *new, strips = pl.pallas_call(
        kernel,
        out_shape=(block, block, block, jax.ShapeDtypeStruct((2, 32, 16, BLOCK), bf16)),
        in_specs=[hbm, hbm, smem, hbm, hbm, hbm, hbm, hbm],
        out_specs=(hbm, hbm, hbm, hbm),
        scratch_shapes=[
            V((TOK, BAND), bf16),
            V((TOK, COLS), bf16),
            V((BAND, TOK), bf16),
            V((NY, PARTS, TOK, HALF), bf16),
            V((8, PARTS, NY * TOK, HALF), bf16),
            V((BAND, NY * TOK), bf16),
            V((8, PARTS, NZ, 64, HALF), bf16),
            V((8, PARTS, 2, 4, 64, HALF), bf16),
            V((16, 2, 32, 128), f32),
            V((2, 32, 16, 128), bf16),
            V((2, 32, 16, 128), bf16),
            V((2, BLOCK, BLOCK), f32),
            V((2, 16, 16, BLOCK), bf16),
            *[V((2, BLOCK, BLOCK), f32)] * 5,
            DMA((N_SEND,)),
            DMA((N_RECV,)),
            DMA((2, 32)),
            DMA((2, 32)),
            DMA((2, 32)),
            DMA((2, 32)),
            DMA((12,)),
        ],
        compiler_params=pltpu.CompilerParams(collective_id=0, has_side_effects=True, vmem_limit_bytes=67_043_328),
        name="shampoo",
    )(
        context, cotangent, block_table,
        left_stat[0], right_stat[0], root_left[0], root_right[0], second_moment[0],
    )
    ln, rn, sn, sd = pl.pallas_call(
        emit,
        out_shape=(block, block, block, jax.ShapeDtypeStruct((16, 8192), bf16)),
        in_specs=[smem, hbm, hbm, hbm, hbm],
        out_specs=(hbm, hbm, hbm, hbm),
        scratch_shapes=[
            *[V((2, BLOCK, BLOCK), f32)] * 3,
            V((2, 32, 16, BLOCK), bf16),
            V((16, 8192), bf16),
            pltpu.SMEM((64,), jnp.int32),
            DMA((4,)),
        ],
        compiler_params=pltpu.CompilerParams(vmem_limit_bytes=67_043_328),
        name="emit",
    )(block_table, *new, strips)
    return ln[None], rn[None], sn[None], sd[None]


def solution(mesh):
    finer = Mesh(mesh.devices.reshape(NZ, NY, NX, 2), ("z", "y", "x", "c"))
    F, T = ("z", "y"), ("x", "c")
    stat = P(T, F, None, None)
    return jax.shard_map(
        per_device,
        mesh=finer,
        in_specs=(P(F, T), P(F, T), P(T, None), stat, stat, stat, stat, stat),
        out_specs=(stat, stat, stat, P(T, F, None)),
        check_vma=False,
    )
```

time: 82.9 us -> 80.6 us (0.972)
  local copies, waits for them, and re-layouts: 5.6 us -> 0 us
  Pallas kernels: 75.7 us -> 79.6 us
    unnamed x12 -> x0, local copies, waits for them, and re-layouts: 5.6 us -> none
    pallas_call x0 -> x1, Pallas kernels: none -> 3.04 us  [per_device(): pl.pallas_call(emit, out_shape=(block, block, block, jax.ShapeDtypeStruct...]
    pallas_call x1, Pallas kernels: 75.7 us -> 76.6 us  [per_device(): pl.pallas_call(kernel, out_shape=(block, block, block, jax.ShapeDtypeStru...]
where the time goes in v3:
time: 80.6 us; the launch traced here: 80.3 us
  Pallas kernels  79.6 us (99%)
    pallas_call x1, Pallas kernels, per_device(): pl.pallas_call(kernel, out_shape=(block, block, block, jax.ShapeDtypeStru...  76.6 us
    pallas_call x1, Pallas kernels, per_device(): pl.pallas_call(emit, out_shape=(block, block, block, jax.ShapeDtypeStruct...  3.04 us

profile of v3, /device:TPU:32, one launch (start us, length us, event | category | flops | bytes accessed | tf_op | source)
XLA Modules:
  0.0 80.3 jit_solution(335912140888243990)
XLA Ops:
  0.6 76.6 %shampoo.1 = (f32[2,256,256]{2,1,0:T(8,128)}, f32[2,256,256]{2,1,0:T(8,128)}, f32[2,256,256]{2,1,0:T(8,128)}, bf16[2,32,16,256]{3,2,1,0:T(8,128)(2,1)}) custom-call(bf16[256,512]{1,0:T(8,128)(2,1)} %ctx_h.1, bf16[256,1024]{1,0:T(8,128)(2,1)} %cot_h.1, s32[1,64]{1,0:T(1,128)} %tbl.3, f32[2,256,256]{2,1,0:T(8,128)} %bitcast.9, f32[2,256,256]{2,1,0:T(8,128)} %bitcast.10, ...), custom_call_target="tpu_custom_call" | custom-call | tf_op jit(solution)/shard_map/shampoo/pallas_call | solution.py:451
  77.2 3.0 %emit.1 = (f32[2,256,256]{2,1,0:T(8,128)}, f32[2,256,256]{2,1,0:T(8,128)}, f32[2,256,256]{2,1,0:T(8,128)}, bf16[16,8192]{1,0:T(8,128)(2,1)}) custom-call(s32[1,64]{1,0:T(1,128)} %tbl.3, f32[2,256,256]{2,1,0:T(8,128)} %get-tuple-element.12.ln_i, f32[2,256,256]{2,1,0:T(8,128)} %get-tuple-element.13.rn_i, f32[2,256,256]{2,1,0:T(8,128)} %get-tuple-element.14.sn_i, ...), custom_call_target="tpu_custom_call" | custom-call | tf_op jit(solution)/shard_map/emit/pallas_call | solution.py:485

commit v4 on v2

--- a/solution.py
+++ b/solution.py
@@ -291,20 +291,26 @@
         )
 
     def each(do):
-        def body(i, carry):
+        def body(k, carry):
+            for i in range(NY):
+                do(k * NY + i)
+            return carry
+
+        lax.fori_loop(0, NZ - 1, body, 0)
+        for i in range(NY * (NZ - 1), NY * NZ - 1):
             do(i)
+
+    for s in range(2):
+
+        def send1(k, carry, s=s, dests=NY):
+            for i in range(dests):
+                out1[s, k * NY + i] = patch(other(k * NY + i)[2], s)
+            for i in range(dests):
+                copy1(k * NY + i, s).start()
             return carry
 
-        lax.fori_loop(0, 31, body, 0)
-
-    for s in range(2):
-
-        def send1(i, s=s):
-            f = other(i)[2]
-            out1[s, i] = patch(f, s)
-            copy1(i, s).start()
-
-        each(send1)
+        lax.fori_loop(0, NZ - 1, send1, 0)
+        send1(NZ - 1, 0, dests=NY - 1)
         in1[s, me] = patch(me, s)
 
     highest = lax.Precision.HIGHEST
@@ -366,6 +372,17 @@
         copy.wait()
 
 
+def emit(*refs):
+    ins, outs, held, sems = refs[:4], refs[4:8], refs[8:12], refs[12]
+    for i in range(4):
+        pltpu.make_async_copy(ins[i], held[i], sems.at[i]).start()
+    for i in range(4):
+        pltpu.make_async_copy(ins[i], held[i], sems.at[i]).wait()
+        pltpu.make_async_copy(held[i], outs[i], sems.at[i]).start()
+    for i in range(4):
+        pltpu.make_async_copy(held[i], outs[i], sems.at[i]).wait()
+
+
 def per_device(context, cotangent, block_table, left_stat, right_stat, root_left, root_right, second_moment):
     ids = jnp.arange(64, dtype=jnp.int32)
     inverse = jnp.sum(jnp.where(block_table[0][None, :] == ids[:, None], ids[None, :], 0), axis=1)[None]
@@ -374,7 +391,8 @@
     block = jax.ShapeDtypeStruct((2, BLOCK, BLOCK), f32)
     V = pltpu.VMEM
     DMA = pltpu.SemaphoreType.DMA
-    ln, rn, sn, sd = pl.pallas_call(
+    shapes = (block, block, block, jax.ShapeDtypeStruct((16, 8192), bf16))
+    made = pl.pallas_call(
         kernel,
         out_shape=(block, block, block, jax.ShapeDtypeStruct((16, 8192), bf16)),
         in_specs=[hbm, hbm, smem, smem, hbm, hbm, hbm, hbm, hbm],
@@ -410,6 +428,15 @@
         context, cotangent, block_table, inverse,
         left_stat[0], right_stat[0], root_left[0], root_right[0], second_moment[0],
     )
+    ln, rn, sn, sd = pl.pallas_call(
+        emit,
+        out_shape=shapes,
+        in_specs=[hbm] * 4,
+        out_specs=(hbm,) * 4,
+        scratch_shapes=[*[V(v.shape, v.dtype) for v in shapes], DMA((4,))],
+        compiler_params=pltpu.CompilerParams(vmem_limit_bytes=67_043_328),
+        name="emit",
+    )(*made)
     return ln[None], rn[None], sn[None], sd[None]
 
 

time: 82.9 us -> 80 us (0.965)
  local copies, waits for them, and re-layouts: 5.6 us -> 0.65 us
  Pallas kernels: 75.7 us -> 77.9 us
    unnamed x12 -> x2, local copies, waits for them, and re-layouts: 5.6 us -> 0.65 us
    pallas_call x0 -> x1, Pallas kernels: none -> 2.3 us  [per_device(): pl.pallas_call(emit, out_shape=shapes, in_specs=[hbm] * 4, out_specs=(hbm...]
where the time goes in v4:
time: 80 us; the launch traced here: 79.8 us
  Pallas kernels  77.9 us (97%)
    pallas_call x1, Pallas kernels, per_device(): pl.pallas_call(kernel, out_shape=(block, block, block, jax.ShapeDtypeStru...  75.6 us
    pallas_call x1, Pallas kernels, per_device(): pl.pallas_call(emit, out_shape=shapes, in_specs=[hbm] * 4, out_specs=(hbm...  2.3 us

profile of v4, /device:TPU:32, one launch (start us, length us, event | category | flops | bytes accessed | tf_op | source)
XLA Modules:
  0.0 79.8 jit_solution(12603345030934253710)
XLA Ops:
  0.6 0.0 copy-start
  0.6 0.6 copy-done
  1.3 0.6 select_reduce_fusion
  1.9 75.6 %shampoo.1 = (f32[2,256,256]{2,1,0:T(8,128)}, f32[2,256,256]{2,1,0:T(8,128)}, f32[2,256,256]{2,1,0:T(8,128)}, bf16[16,8192]{1,0:T(8,128)(2,1)}) custom-call(bf16[256,512]{1,0:T(8,128)(2,1)} %ctx_h.1, bf16[256,1024]{1,0:T(8,128)(2,1)} %cot_h.1, s32[1,64]{1,0:T(1,128)} %tbl.1, s32[1,64]{1,0:T(1,128)} %bitcast.17, f32[2,256,256]{2,1,0:T(8,128)} %bitcast.11, ...), custom_call_target="tpu_custom_call" | custom-call | tf_op jit(solution)/shard_map/shampoo/pallas_call | solution.py:395
  77.5 2.3 %emit.1 = (f32[2,256,256]{2,1,0:T(8,128)}, f32[2,256,256]{2,1,0:T(8,128)}, f32[2,256,256]{2,1,0:T(8,128)}, bf16[16,8192]{1,0:T(8,128)(2,1)}) custom-call(f32[2,256,256]{2,1,0:T(8,128)} %get-tuple-element.12.refs_0_, f32[2,256,256]{2,1,0:T(8,128)} %get-tuple-element.13.refs_1_, f32[2,256,256]{2,1,0:T(8,128)} %get-tuple-element.14.refs_2_, ...), custom_call_target="tpu_custom_call" | custom-call | tf_op jit(solution)/shard_map/emit/pallas_call | solution.py:431
Async XLA Ops:
  0.6 0.7 copy-start

commit v5 on v4

--- a/solution.py
+++ b/solution.py
@@ -74,6 +74,7 @@
 
     y_at = {off: wrap(y + off, NY) for off in (0, 1, -1, 2)}
     xp, xm = wrap(x + 1, NX), wrap(x - 1, NX)
+    x2 = wrap(x + 2, NX)
     zp, zm = wrap(z + 1, NZ), wrap(z - 1, NZ)
 
     load_cot = pltpu.make_async_copy(cot_h, cot, loc.at[9])
@@ -86,7 +87,7 @@
     ]
 
     barrier = pltpu.get_barrier_semaphore()
-    near = [{"y": y_at[off]} for off in PEER_OFF] + [{"x": xp}, {"x": xm}, {"z": zp}, {"z": zm}, {"c": 1 - c}]
+    near = [{"y": y_at[off]} for off in PEER_OFF] + [{"x": xp}, {"x": xm}, {"x": x2}, {"z": zp}, {"z": zm}, {"c": 1 - c}]
     for where in near:
         pl.semaphore_signal(barrier, inc=1, device_id=where, device_id_type=MESH)
 
@@ -114,6 +115,7 @@
     send(pieces.at[0], here, ("Bx", -1, 0), x=xp)
     send(pieces.at[0], here, ("Bx", 1, 0), x=xm)
     send(pieces.at[0], here, ("Bc", 0, 0), c=1 - c)
+    send(pieces.at[0], here, ("Bx2", 0, 0), x=x2)
     for copy in stats:
         copy.start()
 
@@ -153,14 +155,18 @@
         for off, x_at, half, to in ((-1, xm, 0, xp), (1, xp, 1, xm)):
             t = x_at * 2 + c
             arrived(bpart(t, ya), "Bx", off, yi)
-            send(bpart(t, ya, half), bpart(t, ya, half), ("Bx2", half, yi), x=to)
+            if yi:
+                send(bpart(t, ya, half), bpart(t, ya, half), ("Bx2", half, yi), x=to)
             send(bpart(t, ya), bpart(t, ya), ("Bc", off, yi), c=1 - c)
 
     def far(yi):
         t = wrap(x + 2, NX) * 2 + c
         ya = y_at[Y_OFF[yi]]
-        arrived(bpart(t, ya, 0), "Bx2", 0, yi)
-        arrived(bpart(t, ya, 1), "Bx2", 1, yi)
+        if yi:
+            arrived(bpart(t, ya, 0), "Bx2", 0, yi)
+            arrived(bpart(t, ya, 1), "Bx2", 1, yi)
+        else:
+            arrived(bpart(t, ya), "Bx2", 0, 0)
         send(bpart(t, ya), bpart(t, ya), ("Bc", 2, yi), c=1 - c)
 
     def rows_here(k):
@@ -223,6 +229,7 @@
     step(1, 1)
     pass_on(1)
     pass_on(2)
+    far(0)
     rows_here(1)
     for u in (0, 1):
         product(u, 1)
@@ -240,8 +247,8 @@
     for u in (0, 1):
         product(u, 3)
         step(u, 4)
-    for yi in range(NY - 1):
-        far(yi)
+    far(1)
+    far(2)
     for u in (2, 4, 3, 5):
         product(u, 3)
         step(u, 2)

time: 80 us -> 79.7 us (level)
  no operation moved by 1% of the time
where the time goes in v5:
time: 79.7 us; the launch traced here: 79.6 us
  Pallas kernels  77.7 us (97%)
    pallas_call x1, Pallas kernels, per_device(): pl.pallas_call(kernel, out_shape=(block, block, block, jax.ShapeDtypeStru...  75.4 us
    pallas_call x1, Pallas kernels, per_device(): pl.pallas_call(emit, out_shape=shapes, in_specs=[hbm] * 4, out_specs=(hbm...  2.3 us

profile of v5, /device:TPU:32, one launch (start us, length us, event | category | flops | bytes accessed | tf_op | source)
XLA Modules:
  0.0 79.6 jit_solution(8242316827485335771)
XLA Ops:
  0.6 0.0 copy-start
  0.6 0.6 copy-done
  1.3 0.6 select_reduce_fusion
  1.9 75.4 %shampoo.1 = (f32[2,256,256]{2,1,0:T(8,128)}, f32[2,256,256]{2,1,0:T(8,128)}, f32[2,256,256]{2,1,0:T(8,128)}, bf16[16,8192]{1,0:T(8,128)(2,1)}) custom-call(bf16[256,512]{1,0:T(8,128)(2,1)} %ctx_h.1, bf16[256,1024]{1,0:T(8,128)(2,1)} %cot_h.1, s32[1,64]{1,0:T(1,128)} %tbl.1, s32[1,64]{1,0:T(1,128)} %bitcast.17, f32[2,256,256]{2,1,0:T(8,128)} %bitcast.11, ...), custom_call_target="tpu_custom_call" | custom-call | tf_op jit(solution)/shard_map/shampoo/pallas_call | solution.py:402
  77.3 2.3 %emit.1 = (f32[2,256,256]{2,1,0:T(8,128)}, f32[2,256,256]{2,1,0:T(8,128)}, f32[2,256,256]{2,1,0:T(8,128)}, bf16[16,8192]{1,0:T(8,128)(2,1)}) custom-call(f32[2,256,256]{2,1,0:T(8,128)} %get-tuple-element.12.refs_0_, f32[2,256,256]{2,1,0:T(8,128)} %get-tuple-element.13.refs_1_, f32[2,256,256]{2,1,0:T(8,128)} %get-tuple-element.14.refs_2_, ...), custom_call_target="tpu_custom_call" | custom-call | tf_op jit(solution)/shard_map/emit/pallas_call | solution.py:438
Async XLA Ops:
  0.6 0.7 copy-start
